TPU v7x, 128 devices: a whole 4x4x4 slice. The times are simulated.
128 devices in a mesh: row: 8 (over x, z_lo), col: 16 (over z_hi, y, core).
Axes of the slice: x: 4, y: 4, z: 4 (z_hi: 2, z_lo: 2; z = z_hi * 2 + z_lo), core: 2. Of those that a mesh axis runs over, the one named last changes fastest.
Arguments:
- upper_tiles: bfloat16 [1024, 5, 256, 256], P('row', None, 'col'), may hold values from -0.8984375 to 0.8984375
- occupied: int32 [1024, 4], P(('row', 'col')), may hold values from 0 to 1, as said below
Outputs:
- square_tiles: bfloat16 [1024, 5, 256, 256], P('row', None, 'col')
Inputs may be any that keep to these rules, and one draw needn't show every extreme that they name: Occupancy; its density differs between aligned groups of 8 block rows, and the diagonal block is always occupied (not listed).
All inputs are finite; a program needn't handle non-finite values.
Results may differ from a plain program's by a relative error of at most 0.0024.
Values may be sent and summed in bfloat16 or wider, within the bound.
No kernel may reach another device: no remote copies, remote signals or barrier semaphores. Data moves between devices by JAX's collectives and lax.ppermute only.
A program may use at most 256 MiB of HBM per device.

v0:
```python
import jax
import jax.numpy as jnp
from jax import lax
from jax.sharding import PartitionSpec as P


def extended_2(cells, sides, width):
    for axis, dim in sides:
        count = lax.axis_size(axis)
        ends = count - 1
        head = lax.slice_in_dim(cells, 0, width, axis=dim)
        tail = lax.slice_in_dim(cells, cells.shape[dim] - width, cells.shape[dim], axis=dim)
        cells = jnp.concatenate(
            [
                lax.ppermute(tail, axis, [(i, (i + 1) % count) for i in range(ends)]),
                cells,
                lax.ppermute(head, axis, [((i + 1) % count, i) for i in range(ends)]),
            ],
            axis=dim,
        )
    return cells


def build_band(tiles_here, occupied, first_row, total_rows):
    block_rows = occupied.shape[0]
    band_width = occupied.shape[1]
    row_index = first_row + jnp.arange(block_rows, dtype=jnp.int32)
    offsets = jnp.arange(1, band_width + 1, dtype=jnp.int32)
    kept_mask = (occupied == 1) & (row_index[:, None] + offsets[None, :] < total_rows)
    diag_full = tiles_here[:, 0].astype(jnp.float32)
    diag_tile = (0.5 * (diag_full + jnp.swapaxes(diag_full, 1, 2))).astype(jnp.bfloat16)
    off_tiles = jnp.where(
        kept_mask[:, :, None, None], tiles_here[:, 1:], jnp.zeros((), jnp.bfloat16)
    )
    return (jnp.concatenate([diag_tile[:, None], off_tiles], axis=1), kept_mask)


def square_band(extended, kept_mask, block_rows, band_width):
    results = []
    for column_shift in range(band_width + 1):
        lefts = []
        rights = []
        for inner in range(column_shift - band_width, band_width + 1):
            start = band_width + inner
            if inner >= 0:
                left = extended[band_width : band_width + block_rows, inner]
            else:
                left = jnp.swapaxes(extended[start : start + block_rows, -inner], 1, 2)
            rest = column_shift - inner
            if rest >= 0:
                right = extended[start : start + block_rows, rest]
            else:
                lower = band_width + column_shift
                right = jnp.swapaxes(extended[lower : lower + block_rows, -rest], 1, 2)
            lefts.append(left)
            rights.append(right)
        left_stack = jnp.stack(lefts, axis=1)
        right_stack = jnp.stack(rights, axis=1)
        summed = jnp.einsum(
            "rkab,rkbc->rac", left_stack, right_stack, preferred_element_type=jnp.float32
        )
        if column_shift > 0:
            summed = jnp.where(
                kept_mask[:, column_shift - 1, None, None], summed, jnp.zeros((), jnp.float32)
            )
        results.append(summed.astype(jnp.bfloat16))
    return jnp.stack(results, axis=1)


def shards(upper_tiles, occupied):
    tiles_here = lax.all_to_all(upper_tiles, "col", split_axis=0, concat_axis=2, tiled=True)
    block_rows = occupied.shape[0]
    band_width = occupied.shape[1]
    device_count = lax.axis_size("row") * lax.axis_size("col")
    position = lax.axis_index("row") * lax.axis_size("col") + lax.axis_index("col")
    band, kept_mask = build_band(
        tiles_here, occupied, position * block_rows, block_rows * device_count
    )
    extended = extended_2(band, ((("row", "col"), 0),), band_width)
    product = square_band(extended, kept_mask, block_rows, band_width)
    return lax.all_to_all(product, "col", split_axis=2, concat_axis=0, tiled=True)


def solution(mesh):
    return jax.shard_map(
        shards,
        mesh=mesh,
        in_specs=(P("row", None, "col", None), P(("row", "col"), None)),
        out_specs=P("row", None, "col", None),
        check_vma=False,
    )
```

profile of v0, /device:TPU:34, one launch (start us, length us, event | category | flops | bytes accessed | tf_op | source)
XLA Modules:
  0.0 368.4 jit_solution(5053855794059885727)
XLA Ops:
  0.0 7.2 %all-to-all-start = ((bf16[128,5,16,256]{3,2,1,0:T(8,128)(2,1)}), bf16[128,5,16,256]{3,2,1,0:T(8,128)(2,1)}, u32[]{:S(2)}, u32[]{:S(2)}) async-start(bf16[128,5,16,256]{3,2,1,0:T(8,128)(2,1)} %param.2), calls=%async_computation | async-start | bytes 10485760 | tf_op jit(solution)/shard_map/all_to_all | solution.py:71
  7.3 70.3 %all-to-all-done = bf16[128,5,16,256]{3,2,1,0:T(8,128)(2,1)} async-done(((bf16[128,5,16,256]{3,2,1,0:T(8,128)(2,1)}), bf16[128,5,16,256]{3,2,1,0:T(8,128)(2,1)}, u32[]{:S(2)}, u32[]{:S(2)}) %all-to-all-start) | async-done | bytes 5242912 | tf_op jit(solution)/shard_map/all_to_all | solution.py:71
  77.6 3.2 copy.102
  83.1 2.9 copy_select_fusion
  86.0 6.2 %copy.107 = bf16[8,4,256,256]{2,3,0,1:T(8,128)(2,1)} copy(bf16[8,4,256,256]{3,2,0,1:T(8,128)(2,1)} %copy_select_fusion) | data formatting | bytes 8388608 | tf_op jit(solution)/shard_map/jit(_where)/select_n | solution.py:32
  97.1 2.6 fusion.17
  99.7 2.5 collective-permute-start.1
  105.5 26.0 %collective-permute-done.1 = bf16[4,5,256,256]{2,3,0,1:T(8,128)(2,1)S(1)} collective-permute-done((bf16[4,5,256,256]{2,3,0,1:T(8,128)(2,1)S(1)}, bf16[4,5,256,256]{2,3,0,1:T(8,128)(2,1)S(1)}, u32[]{:S(2)}, u32[]{:S(2)}) %collective-permute-start.1) | collective-permute-done | bytes 2621472 | tf_op jit(solution)/shard_map/ppermute | solution.py:17
  131.4 5.9 %collective-permute-done = bf16[4,5,256,256]{2,3,0,1:T(8,128)(2,1)S(1)} collective-permute-done((bf16[4,5,256,256]{2,3,0,1:T(8,128)(2,1)S(1)}, bf16[4,5,256,256]{2,3,0,1:T(8,128)(2,1)S(1)}, u32[]{:S(2)}, u32[]{:S(2)}) %collective-permute-start) | collective-permute-done | bytes 2621472 | tf_op jit(solution)/shard_map/ppermute | solution.py:15
  146.6 4.0 %fusion.51 = (bf16[8,1,256,256]{2,3,0,1:T(8,128)(2,1)}, bf16[8,1,256,256]{3,2,0,1:T(8,128)(2,1)}, bf16[8,1,256,256]{3,2,0,1:T(8,128)(2,1)}, bf16[8,7,256,256]{2,...) fusion(bf16[12,5,256,256]{2,3,0,1:T(8,128)(2,1)S(1)} %get-tuple, ...), kind=kLoop, calls=%fused_computation.112 | loop fusion | bytes 20971520 | tf_op jit(solution)/shard_map/slice | solution.py:51
  157.4 2.3 copy.111
  162.0 3.1 constant_dynamic-update-slice_fusion.15
  165.0 3.1 constant_dynamic-update-slice_fusion.14
  168.1 2.3 constant_dynamic-update-slice_fusion.2
  183.1 2.3 constant_dynamic-update-slice_fusion.18
  185.4 2.3 constant_dynamic-update-slice_fusion.17
  187.7 4.4 %slice_dynamic-update-slice_fusion.8 = (bf16[8,6,256,256]{3,2,0,1:T(8,128)(2,1)}, bf16[8,1,256,256]{2,3,0,1:T(8,128)(2,1)}, bf16[8,8,256,256]{3,2,0,1:T(8,128)(2...) fusion(bf16[8,6,256,256]{3,2,0,1:T(8,128)(2,1)} %constant_dynamic-u, ...), kind=kLoop, calls=%fused_computation.68 | loop fusion | bytes 9437184
  198.9 2.4 constant_dynamic-update-slice_fusion.10
  211.1 2.3 bitcast_dynamic-update-slice_fusion.6
  217.0 6.0 %slice_dynamic-update-slice_fusion = (bf16[8,5,256,256]{2,3,0,1:T(8,128)(2,1)}, bf16[8,7,256,256]{2,3,0,1:T(8,128)(2,1)}, bf16[8,1,256,256]{2,3,0,1:T(8,128)(2,1...) fusion(bf16[8,5,256,256]{2,3,0,1:T(8,128)(2,1)} %get-tuple-elem, ...), kind=kLoop, calls=%fused_computation.49 | loop fusion | bytes 14680064 | tf_op jit(solution)/shard_map/stack | solution.py:58
  230.4 2.4 constant_dynamic-update-slice_fusion.16
  239.4 3.1 bitcast_dynamic-update-slice_fusion
  249.6 5.9 %constant_dynamic-update-slice_fusion.12 = (bf16[8,8,256,256]{3,2,0,1:T(8,128)(2,1)}, bf16[8,9,256,256]{3,2,0,1:T(8,128)(2,1)}) fusion(bf16[8,8,256,256]{3,2,0,1:T(8,128)(2,1)} %get-tuple-element.43, bf16[8,9,256,256]{3,2,0,1:T(8,128)(2,1)} %get-tuple-element.45, pred[8,4]{0,1:T(4,128)(4,1)S(1)} %fusion.47, bf16[8,5,256,256]{3,2,1,0:T(8,128)(2,1)} %bitcast.187), kind=kLoop, calls=%fused_computation.84 | loop fusion | flops 2097152 | bytes 12582944 | tf_op jit(solution)/shard_map/stack | solution.py:57
  255.5 9.0 %fusion.29 = bf16[8,5,256,256]{3,2,0,1:T(8,128)(2,1)S(1)} fusion(bf16[8,9,256,256]{3,2,0,1:T(8,128)(2,1)} %get-tuple-element.42, bf16[8,9,256,256]{3,2,0,1:T(8,128)(2,1)} %bitcast_dynamic-update-slice_fusion.6), kind=kOutput, calls=%fused_computation.39 | convolution fusion | flops 2416443392 | bytes 19922944 | tf_op jit(solution)/shard_map/rkab,rkbc->rac/dot_general | solution.py:59
  265.6 8.2 %fusion.31 = bf16[8,5,256,256]{3,2,0,1:T(8,128)(2,1)S(1)} fusion(bf16[8,5,256,256]{3,2,0,1:T(8,128)(2,1)S(1)} %fusion.29, bf16[8,8,256,256]{3,2,0,1:T(8,128)(2,1)} %get-tuple-element.41, bf16[8,8,256,256]{3,2,0,1:T(8,128)(2,1)} %bitcast_dynamic-update-slice_fusion.3, pred[8]{0:T(512)(128)(4,1)S(1)} %get-tuple-element.49), kind=kOutput, calls=%fused_computation.41 | convolution fusion | flops 2148532224 | bytes 17826304 | tf_op jit(solution)/shard_map/rkab,rkbc->rac/dot_general | solution.py:59
  273.8 4.4 %fusion.35 = bf16[8,5,256,256]{3,2,0,1:T(8,128)(2,1)S(1)} fusion(bf16[8,5,256,256]{3,2,0,1:T(8,128)(2,1)S(1)} %fusion.31, bf16[8,7,256,256]{2,3,0,1:T(8,128)(2,1)} %bitcast_dynamic-update-slice_fusion.1, bf16[8,4,256,256]{3,2,0,1:T(8,128)(2,1)S(1)} %copy-done.5, bf16[8,1,256,256]{3,2,0,1:T(8,128)(2,1)S(1)} %fusion.46, ...), kind=kOutput, calls=%fused_computation.43 | convolution fusion | flops 1891106816 | bytes 15729152 | tf_op jit(solution)/shard_map/rkab,rkbc->rac/dot_general | solution.py:59
  278.3 2.3 copy-done.6
  280.6 5.7 %fusion.41 = bf16[8,5,256,256]{3,2,0,1:T(8,128)(2,1)} fusion(bf16[8,5,256,256]{3,2,0,1:T(8,128)(2,1)} %copy-done.6, bf16[8,6,256,256]{3,2,0,1:T(8,128)(2,1)} %get-tuple-element.12, bf16[8,4,256,256]{3,2,0,1:T(8,128)(2,1)S(1)} %copy-done.5, bf16[8,1,256,256]{3,2,0,1:T(8,128)(2,1)S(1)} %fusion.46, bf16[8,1,256,256]{3,2,0,1:T(8,128)(2,1)S(1)} %copy-done.11, ...), kind=kOutput, calls=%fused_computation.45 | convolution fusion | flops 1617952768 | bytes 13631496 | tf_op jit(solution)/shard_map/rkab,rkbc->rac/dot_general | solution.py:59
  286.3 5.4 %fusion.45 = bf16[8,5,256,256]{3,2,0,1:T(8,128)(2,1)} fusion(bf16[8,5,256,256]{3,2,0,1:T(8,128)(2,1)} %fusion.41, bf16[8,5,256,256]{2,3,0,1:T(8,128)(2,1)} %get-tuple-element.5, bf16[8,1,256,256]{2,3,0,1:T(8,128)(2,1)S(1)} %copy.106, bf16[8,4,256,256]{2,3,0,1:T(8,128)(2,1)S(1)} %copy-done.3, pred[8]{0:T(512)(128)(4,1)S(1)} %get-tuple-element.46), kind=kOutput, calls=%fused_computation.47 | convolution fusion | flops 1345847296 | bytes 11534344 | tf_op jit(solution)/shard_map/rkab,rkbc->rac/dot_general | solution.py:59
  291.7 5.5 %copy.130 = bf16[8,5,256,256]{3,0,1,2:T(8,128)(2,1)S(1)} copy(bf16[8,5,256,256]{3,2,0,1:T(8,128)(2,1)} %fusion.45) | data formatting | bytes 10485760 | tf_op jit(solution)/shard_map/stack | solution.py:67
  297.2 67.4 %all_to_all.36 = bf16[8,5,256,256]{3,0,1,2:T(8,128)(2,1)S(1)} all-to-all(bf16[8,5,256,256]{3,0,1,2:T(8,128)(2,1)S(1)} %copy.130), channel_id=1, replica_groups=mesh['row'=8,'col'=16] {'col'}, dimensions={2} | all-to-all | bytes 10485760 | tf_op jit(solution)/shard_map/all_to_all | solution.py:81
  364.6 3.8 %copy.131 = bf16[16,8,5,16,256]{4,3,2,1,0:T(8,128)(2,1)} copy(bf16[16,8,5,16,256]{4,1,2,3,0:T(8,128)(2,1)S(1)} %bitcast.188) | data formatting | bytes 10485760 | tf_op jit(solution)/shard_map/all_to_all | solution.py:81
  (78 shorter events, 83.8 us)
Async XLA Ops:
  0.0 7.2 %copy-start.13 = (s32[8,4]{0,1:T(4,128)S(1)}, s32[8,4]{0,1:T(4,128)}, u32[]{:S(2)}) copy-start(s32[8,4]{0,1:T(4,128)} %param.3) | copy-start | bytes 388
  0.0 77.6 %all-to-all-start = ((bf16[128,5,16,256]{3,2,1,0:T(8,128)(2,1)}), bf16[128,5,16,256]{3,2,1,0:T(8,128)(2,1)}, u32[]{:S(2)}, u32[]{:S(2)}) async-start(bf16[128,5,16,256]{3,2,1,0:T(8,128)(2,1)} %param.2), calls=%async_computation | async-start | bytes 10485760 | tf_op jit(solution)/shard_map/all_to_all | solution.py:71
  80.8 2.3 copy-start.4
  97.1 7.3 %copy-start.2 = (bf16[8,4,256,256]{2,3,0,1:T(8,128)(2,1)S(1)}, bf16[8,4,256,256]{2,3,0,1:T(8,128)(2,1)}, u32[]{:S(2)}) copy-start(bf16[8,4,256,256]{2,3,0,1:T(8,128)(2,1)} %copy.107) | copy-start | bytes 12582916
  99.7 31.7 %collective-permute-start.1 = (bf16[4,5,256,256]{2,3,0,1:T(8,128)(2,1)S(1)}, bf16[4,5,256,256]{2,3,0,1:T(8,128)(2,1)S(1)}, u32[]{:S(2)}, u32[]{:S(2)}) collective-permute-start(bf16[4,5,256,256]{2,3,0,1:T(8,128)(2,1)S(1)} %get-tuple-element.33), channel_id=1, source_target_pairs={{1,0},{2,1},{3,2},{4,3},{5,4},{6,5},{7,6},{8,7},{9,8},{10,9},{11,1... | collective-permute-start | bytes 7864328 | tf_op jit(solution)/shard_map/ppermute | solution.py:17
  102.3 35.1 %collective-permute-start = (bf16[4,5,256,256]{2,3,0,1:T(8,128)(2,1)S(1)}, bf16[4,5,256,256]{2,3,0,1:T(8,128)(2,1)S(1)}, u32[]{:S(2)}, u32[]{:S(2)}) collective-permute-start(bf16[4,5,256,256]{2,3,0,1:T(8,128)(2,1)S(1)} %get-tuple-element.34), channel_id=1, source_target_pairs={{0,1},{1,2},{2,3},{3,4},{4,5},{5,6},{6,7},{7,8},{8,9},{9,10},{10,1... | collective-permute-start | bytes 7864328 | tf_op jit(solution)/shard_map/ppermute | solution.py:15
  139.1 11.5 %copy-start = (bf16[12,5,256,256]{2,3,0,1:T(8,128)(2,1)}, bf16[12,5,256,256]{2,3,0,1:T(8,128)(2,1)S(1)}, u32[]{:S(2)}) copy-start(bf16[12,5,256,256]{2,3,0,1:T(8,128)(2,1)S(1)} %get-tuple-element.32) | copy-start | bytes 23592964
  139.1 11.4 %copy-start.1 = (bf16[12,5,256,256]{2,3,0,1:T(8,128)(2,1)}, bf16[12,5,256,256]{2,3,0,1:T(8,128)(2,1)S(1)}, u32[]{:S(2)}) copy-start(bf16[12,5,256,256]{2,3,0,1:T(8,128)(2,1)S(1)} %get-tuple-element.31) | copy-start | bytes 23592964
  198.9 8.9 %copy-start.9 = (bf16[8,1,256,256]{3,2,0,1:T(8,128)(2,1)S(1)}, bf16[8,1,256,256]{3,2,0,1:T(8,128)(2,1)}, u32[]{:S(2)}) copy-start(bf16[8,1,256,256]{3,2,0,1:T(8,128)(2,1)} %copy.113) | copy-start | bytes 3145732
  198.9 10.0 %copy-start.8 = (bf16[8,1,256,256]{3,2,0,1:T(8,128)(2,1)S(1)}, bf16[8,1,256,256]{3,2,0,1:T(8,128)(2,1)}, u32[]{:S(2)}) copy-start(bf16[8,1,256,256]{3,2,0,1:T(8,128)(2,1)} %copy.114) | copy-start | bytes 3145732
  198.9 11.0 %copy-start.7 = (bf16[8,1,256,256]{3,2,0,1:T(8,128)(2,1)S(1)}, bf16[8,1,256,256]{3,2,0,1:T(8,128)(2,1)}, u32[]{:S(2)}) copy-start(bf16[8,1,256,256]{3,2,0,1:T(8,128)(2,1)} %copy.115) | copy-start | bytes 3145732
  230.4 8.0 %copy-start.10 = (bf16[8,1,256,256]{3,2,0,1:T(8,128)(2,1)S(1)}, bf16[8,1,256,256]{3,2,0,1:T(8,128)(2,1)}, u32[]{:S(2)}) copy-start(bf16[8,1,256,256]{3,2,0,1:T(8,128)(2,1)} %copy.140) | copy-start | bytes 3145732
  265.6 8.3 %copy-start.5 = (bf16[8,4,256,256]{3,2,0,1:T(8,128)(2,1)S(1)}, bf16[8,4,256,256]{3,2,0,1:T(8,128)(2,1)}, u32[]{:S(2)}) copy-start(bf16[8,4,256,256]{3,2,0,1:T(8,128)(2,1)} %copy_select_fusion) | copy-start | bytes 12582916
  265.6 8.3 %copy-start.11 = (bf16[8,1,256,256]{3,2,0,1:T(8,128)(2,1)S(1)}, bf16[8,1,256,256]{3,2,0,1:T(8,128)(2,1)}, u32[]{:S(2)}) copy-start(bf16[8,1,256,256]{3,2,0,1:T(8,128)(2,1)} %get-tuple-element.16) | copy-start | bytes 3145732
  265.6 8.3 %copy-start.12 = (bf16[8,1,256,256]{3,2,0,1:T(8,128)(2,1)S(1)}, bf16[8,1,256,256]{3,2,0,1:T(8,128)(2,1)}, u32[]{:S(2)}) copy-start(bf16[8,1,256,256]{3,2,0,1:T(8,128)(2,1)} %get-tuple-element.15) | copy-start | bytes 3145732
  278.3 2.3 copy-start.6
  280.6 5.7 %copy-start.3 = (bf16[8,4,256,256]{2,3,0,1:T(8,128)(2,1)S(1)}, bf16[8,4,256,256]{2,3,0,1:T(8,128)(2,1)}, u32[]{:S(2)}) copy-start(bf16[8,4,256,256]{2,3,0,1:T(8,128)(2,1)} %copy.107) | copy-start | bytes 12582916
where the time goes:
time: 373 us; the launch traced here: 368 us
  local copies, waits for them, and re-layouts  139 us (37%)
  waiting for transfers between devices  102 us (27%)
  blocking collectives  67.4 us (18%)
  matrix products  32.8 us (9%)
  other arithmetic  15.2 us (4%)
  starting transfers between devices  11.8 us (3%)
    unnamed x62, local copies, waits for them, and re-layouts  72.3 us
    all_to_all x1, waiting for transfers between devices, shards(): lax.all_to_all(upper_tiles, 'col', split_axis=0, concat_axis=2, tiled=True)  70.3 us
    all_to_all x1, blocking collectives, shards(): lax.all_to_all(product, 'col', split_axis=2, concat_axis=0, tiled=True)  67.4 us
    dot_general x5, matrix products, square_band(): jnp.einsum('rkab,rkbc->rac', left_stack, right_stack, preferred_element_t...  32.8 us
    ppermute x1, waiting for transfers between devices, extended_2(): lax.ppermute(head, axis, [((i + 1) % count, i) for i in range(ends)])  26 us
    another operation x8, local copies, waits for them, and re-layouts, square_band(): right_stack = jnp.stack(rights, axis=1)  21.5 us
    slice x5, local copies, waits for them, and re-layouts, square_band(): right = extended[start:start + block_rows, rest]  12.1 us
    slice x4, local copies, waits for them, and re-layouts, square_band(): left = jnp.swapaxes(extended[start:start + block_rows, -inner], 1, 2)  9.16 us
  transfers between devices with their start and end apart: 3, of which 3 were waited for; matrix products, arithmetic and copies ran while one was open for 0% of the time, Pallas kernels for 0%

commit v1 on v0

v1 whole, which is shorter than its diff:
```python
import jax
import jax.numpy as jnp
from jax import lax
from jax.experimental import pallas as pl
from jax.experimental.pallas import tpu as pltpu
from jax.sharding import PartitionSpec as P

AXES = ("row", "col")
BLOCK = 256
BAND = 4
LANES = (2 * BAND + 1) * BLOCK
BELOW = [(m, d) for m in range(1, BAND + 1) for d in range(m, BAND + 1)]
ABOVE = [(m, d) for m in range(BAND) for d in range(BAND - m)]


def halo_kernel(tiles, to_next, to_last, sem):
    rows = tiles.shape[1]
    copies = []
    start = 0
    for m in range(1, BAND + 1):
        count = BAND + 1 - m
        copies.append(
            (tiles.at[:, rows - m, pl.ds(m, count)], to_next.at[:, pl.ds(start, count)])
        )
        start += count
    start = 0
    for m in range(BAND):
        count = BAND - m
        copies.append((tiles.at[:, m, pl.ds(0, count)], to_last.at[:, pl.ds(start, count)]))
        start += count
    started = [
        pltpu.make_async_copy(source, target, sem.at[n])
        for n, (source, target) in enumerate(copies)
    ]
    for copy in started:
        copy.start()
    for copy in started:
        copy.wait()


def halo_tiles(tiles):
    parts, _, _, height, width = tiles.shape
    anywhere = pl.BlockSpec(memory_space=pl.ANY)
    shape = jax.ShapeDtypeStruct((parts, len(BELOW), height, width), tiles.dtype)
    return pl.pallas_call(
        halo_kernel,
        out_shape=(shape, shape),
        in_specs=[anywhere],
        out_specs=(anywhere, anywhere),
        scratch_shapes=[pltpu.SemaphoreType.DMA((2 * BAND,))],
    )(tiles)


def square_kernel(kept, kept_below, kept_above, tiles, below, above, out, strips, done, sem, out_sem):
    rows = tiles.shape[1]
    parts, height = tiles.shape[0], tiles.shape[3]

    def offsets(row):
        if row < 0:
            return [d for m, d in BELOW if m == -row]
        if row >= rows:
            return [d for m, d in ABOVE if m == row - rows]
        return list(range(BAND + 1))

    def stored(row, d):
        if row < 0:
            return below.at[:, BELOW.index((-row, d))]
        if row >= rows:
            return above.at[:, ABOVE.index((row - rows, d))]
        return tiles.at[:, row, d]

    def flag(row, d):
        if row < 0:
            return kept_below[BAND + row, d - 1]
        if row >= rows:
            return kept_above[row - rows, d - 1]
        return kept[row, d - 1]

    def block(row, d):
        return strips.at[BAND + row, :, :, pl.ds((BAND + d) * BLOCK, BLOCK)]

    def load(row, d):
        return pltpu.make_async_copy(stored(row, d), block(row, d), sem.at[BAND + row, d])

    def get(row, d):
        return block(row, d)[...].reshape(BLOCK, BLOCK)

    def put(row, d, value):
        block(row, d)[...] = value.reshape(parts, height, BLOCK)

    for row in range(-BAND, rows + BAND):
        for d in offsets(row):
            load(row, d).start()

    ready = set()

    def arrive(row):
        if row in ready:
            return
        ready.add(row)
        for d in offsets(row):
            load(row, d).wait()
            if d > 0:

                @pl.when(flag(row, d) == 0)
                def _():
                    put(row, d, jnp.zeros((BLOCK, BLOCK), jnp.bfloat16))

    def prepare(j):
        for k in range(j - BAND, j + 1):
            arrive(k)
        raw = get(j, 0)
        both = raw.astype(jnp.float32) + raw.T.astype(jnp.float32)
        put(j, 0, (0.5 * both).astype(jnp.bfloat16))
        for m in range(1, BAND + 1):
            put(j, -m, get(j - m, m).T)

    def store(i, e):
        return pltpu.make_async_copy(done.at[i, e], out.at[:, i, e], out_sem)

    for j in range(BAND):
        prepare(j)
    for i in range(rows):
        prepare(i + BAND)
        for e in range(BAND + 1):
            depth = LANES - e * BLOCK
            left = strips[BAND + i, :, :, pl.ds(e * BLOCK, depth)].reshape(BLOCK, depth)
            right = strips[BAND + i + e, :, :, pl.ds(0, depth)].reshape(BLOCK, depth)
            summed = lax.dot_general(
                left, right, (((1,), (1,)), ((), ())), preferred_element_type=jnp.float32
            )
            if e > 0:
                summed = jnp.where(kept[i, e - 1] != 0, summed, 0.0)
            done[i, e] = summed.astype(jnp.bfloat16).reshape(parts, height, BLOCK)
            store(i, e).start()
    for i in range(rows):
        for e in range(BAND + 1):
            store(i, e).wait()


def square_band(kept, kept_below, kept_above, tiles, below, above):
    parts, rows, width, height, _ = tiles.shape
    scalars = pl.BlockSpec(memory_space=pltpu.SMEM)
    anywhere = pl.BlockSpec(memory_space=pl.ANY)
    return pl.pallas_call(
        square_kernel,
        out_shape=jax.ShapeDtypeStruct(tiles.shape, jnp.bfloat16),
        in_specs=[scalars] * 3 + [anywhere] * 3,
        out_specs=anywhere,
        scratch_shapes=[
            pltpu.VMEM((rows + 2 * BAND, parts, height, LANES), jnp.bfloat16),
            pltpu.VMEM((rows, width, parts, height, BLOCK), jnp.bfloat16),
            pltpu.SemaphoreType.DMA((rows + 2 * BAND, width)),
            pltpu.SemaphoreType.DMA,
        ],
        compiler_params=pltpu.CompilerParams(vmem_limit_bytes=48 << 20),
    )(kept, kept_below, kept_above, tiles, below, above)


def shards(upper_tiles, occupied):
    parts = lax.axis_size("col")
    count = lax.axis_size("row") * parts
    rows, band = occupied.shape
    position = lax.axis_index("row") * parts + lax.axis_index("col")
    index = position * rows + jnp.arange(rows, dtype=jnp.int32)
    offsets = jnp.arange(1, band + 1, dtype=jnp.int32)
    inside = index[:, None] + offsets[None, :] < rows * count
    kept = ((occupied == 1) & inside).astype(jnp.int32)
    forward = [(p, p + 1) for p in range(count - 1)]
    backward = [(p + 1, p) for p in range(count - 1)]
    kept_below = lax.ppermute(kept[rows - BAND :], AXES, forward)
    kept_above = lax.ppermute(kept[:BAND], AXES, backward)
    tiles = upper_tiles.reshape((parts, rows) + upper_tiles.shape[1:])
    tiles = lax.all_to_all(tiles, "col", 0, 0, tiled=True)
    to_next, to_last = halo_tiles(tiles)
    below = lax.ppermute(to_next, AXES, forward)
    above = lax.ppermute(to_last, AXES, backward)
    product = square_band(kept, kept_below, kept_above, tiles, below, above)
    product = lax.all_to_all(product, "col", 0, 0, tiled=True)
    return product.reshape(upper_tiles.shape)


def solution(mesh):
    return jax.shard_map(
        shards,
        mesh=mesh,
        in_specs=(P("row", None, "col", None), P(("row", "col"), None)),
        out_specs=P("row", None, "col", None),
        check_vma=False,
    )
```

time: 373 us -> 266 us (0.71); the launches traced: 368 us -> 266 us
  local copies, waits for them, and re-layouts: 139 us -> 2.45 us
  Pallas kernels: 0 us -> 98.1 us
  waiting for transfers between devices: 102 us -> 10.9 us
  blocking collectives: 67.4 us -> 142 us
  matrix products: 32.8 us -> 0 us
  other arithmetic: 15.2 us -> 0.08 us
    pallas_call x0 -> x2, Pallas kernels: none -> 98.1 us  [the longest x1 80.6 us: halo_tiles(): pl.pallas_call(halo_kernel, out_shape=(shape, shape), in_specs=[anywhere]...]
    all_to_all x1 -> x2, blocking collectives: 67.4 us -> 142 us  [the longest x1 72.3 us: shards(): product = lax.all_to_all(product, 'col', 0, 0, tiled=True)]
    all_to_all x1 -> x0, waiting for transfers between devices: 70.3 us -> none  [shards(): lax.all_to_all(upper_tiles, 'col', split_axis=0, concat_axis=2, tiled=True)]
    unnamed x62 -> x4, local copies, waits for them, and re-layouts: 72.3 us -> 2.44 us
    dot_general x5 -> x0, matrix products: 32.8 us -> none  [square_band(): jnp.einsum('rkab,rkbc->rac', left_stack, right_stack, preferred_element_t...]
    another operation x9 -> x0, local copies, waits for them, and re-layouts: 27 us -> none  [the longest x8 21.5 us: square_band(): right_stack = jnp.stack(rights, axis=1)]
    slice x12 -> x1, local copies, waits for them, and re-layouts: 24 us -> 0.01 us  [shards(): kept_above = lax.ppermute(kept[:BAND], AXES, backward)]
    ppermute x2 -> x4, waiting for transfers between devices: 31.9 us -> 10.9 us  [the longest x1 10.9 us: shards(): kept_above = lax.ppermute(kept[:BAND], AXES, backward)]
  transfers between devices with their start and end apart: 3 -> 4, of which waited for: 3 -> 1; matrix products, arithmetic and copies ran while one was open for 0% -> 0% of each run, Pallas kernels for 0% -> 0%
where the time goes in v1:
time: 266 us
  blocking collectives  142 us (53%)
  Pallas kernels  98.1 us (37%)
  starting transfers between devices  12 us (5%)
  waiting for transfers between devices  10.9 us (4%)
    pallas_call x1, Pallas kernels, halo_tiles(): pl.pallas_call(halo_kernel, out_shape=(shape, shape), in_specs=[anywhere]...  80.6 us
    all_to_all x1, blocking collectives, shards(): product = lax.all_to_all(product, 'col', 0, 0, tiled=True)  72.3 us
    all_to_all x1, blocking collectives, shards(): tiles = lax.all_to_all(tiles, 'col', 0, 0, tiled=True)  70 us
    pallas_call x1, Pallas kernels, square_band(): pl.pallas_call(square_kernel, out_shape=jax.ShapeDtypeStruct(tiles.shape,...  17.5 us
    ppermute x1, waiting for transfers between devices, shards(): kept_above = lax.ppermute(kept[:BAND], AXES, backward)  10.9 us
    ppermute x1, starting transfers between devices, shards(): above = lax.ppermute(to_last, AXES, backward)  5.75 us
  transfers between devices with their start and end apart: 4, of which 1 were waited for; matrix products, arithmetic and copies ran while one was open for 0% of the time, Pallas kernels for 0%

profile of v1, /device:TPU:34, one launch (start us, length us, event | category | flops | bytes accessed | tf_op | source)
XLA Modules:
  0.0 265.9 jit_solution(17304779495911503895)
XLA Ops:
  0.0 70.0 %all_to_all.10.tiles = bf16[16,8,5,16,256]{4,3,2,1,0:T(8,128)(2,1)} all-to-all(bf16[16,8,5,16,256]{4,3,2,1,0:T(8,128)(2,1)} %bitcast.3), channel_id=1, replica_groups=mesh['row'=8,'col'=16] {'col'}, dimensions={0} | all-to-all | bytes 10485760 | tf_op jit(solution)/shard_map/all_to_all | solution.py:174
  70.0 0.0 copy-start
  70.0 80.6 %shard_map.28 = (bf16[16,10,16,256]{3,2,1,0:T(8,128)(2,1)}, bf16[16,10,16,256]{3,2,1,0:T(8,128)(2,1)}) custom-call(bf16[16,8,5,16,256]{4,3,2,1,0:T(8,128)(2,1)} %all_to_all.10.tiles), custom_call_target="tpu_custom_call" | custom-call | tf_op jit(solution)/shard_map/pallas_call | solution.py:45
  150.6 1.9 collective-permute-start.2
  152.5 5.8 %collective-permute-start.3 = (bf16[16,10,16,256]{3,2,1,0:T(8,128)(2,1)}, bf16[16,10,16,256]{3,2,1,0:T(8,128)(2,1)S(1)}, u32[]{:S(2)}, u32[]{:S(2)}) collective-permute-start(bf16[16,10,16,256]{3,2,1,0:T(8,128)(2,1)} %get-tuple-element.8), channel_id=1, source_target_pairs={{1,0},{2,1},{3,2},{4,3},{5,4},{6,5},{7,6},{8,7},{9,8},{10,9},{11,1... | collective-permute-start | bytes 3932168 | tf_op jit(solution)/shard_map/ppermute | solution.py:177
  158.3 0.0 copy-done
  158.3 0.1 copy.3
  158.4 0.1 fusion.1.kept
  158.5 1.9 collective-permute-start.1
  160.4 2.4 collective-permute-start
  162.8 10.9 %collective-permute-done.1.kept_above = s32[4,4]{1,0:T(4,128)S(1)} collective-permute-done((s32[4,4]{1,0:T(4,128)S(1)}, s32[4,4]{1,0:T(4,128)S(1)}, u32[]{:S(2)}, u32[]{:S(2)}) %collective-permute-start.1) | collective-permute-done | bytes 96 | tf_op jit(solution)/shard_map/ppermute | solution.py:172
  173.7 0.0 collective-permute-done.kept_below
  173.7 0.0 collective-permute-done.2.below
  173.7 0.0 collective-permute-done.3.above
  173.7 17.5 %shard_map.29 = bf16[16,8,5,16,256]{4,3,2,1,0:T(8,128)(2,1)} custom-call(s32[8,4]{1,0:T(8,128)S(1)} %fusion.1.kept, s32[4,4]{1,0:T(4,128)S(1)} %collective-permute-done.kept_below, s32[4,4]{1,0:T(4,128)S(1)} %collective-permute-done.1.kept_above, bf16[16,8,5,16,256]{4,3,2,1,0:T(8,128)(2,1)} %all_to_all.10.tiles, ...), custom_call_target="tpu_custom_call" | custom-call | tf_op jit(solution)/shard_map/pallas_call | solution.py:145
  191.2 72.3 %all_to_all.11 = bf16[16,8,5,16,256]{4,3,2,1,0:T(8,128)(2,1)S(1)} all-to-all(bf16[16,8,5,16,256]{4,3,2,1,0:T(8,128)(2,1)} %shard_map.29), channel_id=1, replica_groups=mesh['row'=8,'col'=16] {'col'}, dimensions={0} | all-to-all | bytes 10485760 | tf_op jit(solution)/shard_map/all_to_all | solution.py:179
  263.5 2.4 copy.5
  (3 shorter events, 0.0 us)
Async XLA Ops:
  70.0 88.3 %copy-start = (s32[8,4]{0,1:T(4,128)S(1)}, s32[8,4]{0,1:T(4,128)}, u32[]{:S(2)}) copy-start(s32[8,4]{0,1:T(4,128)} %param.3) | copy-start | bytes 388
  150.6 23.1 %collective-permute-start.2 = (bf16[16,10,16,256]{3,2,1,0:T(8,128)(2,1)}, bf16[16,10,16,256]{3,2,1,0:T(8,128)(2,1)S(1)}, u32[]{:S(2)}, u32[]{:S(2)}) collective-permute-start(bf16[16,10,16,256]{3,2,1,0:T(8,128)(2,1)} %get-tuple-element.7), channel_id=1, source_target_pairs={{0,1},{1,2},{2,3},{3,4},{4,5},{5,6},{6,7},{7,8},{8,9},{9,10},{10,1... | collective-permute-start | bytes 3932168 | tf_op jit(solution)/shard_map/ppermute | solution.py:176
  152.5 21.2 %collective-permute-start.3 = (bf16[16,10,16,256]{3,2,1,0:T(8,128)(2,1)}, bf16[16,10,16,256]{3,2,1,0:T(8,128)(2,1)S(1)}, u32[]{:S(2)}, u32[]{:S(2)}) collective-permute-start(bf16[16,10,16,256]{3,2,1,0:T(8,128)(2,1)} %get-tuple-element.8), channel_id=1, source_target_pairs={{1,0},{2,1},{3,2},{4,3},{5,4},{6,5},{7,6},{8,7},{9,8},{10,9},{11,1... | collective-permute-start | bytes 3932168 | tf_op jit(solution)/shard_map/ppermute | solution.py:177
  158.5 15.2 %collective-permute-start.1 = (s32[4,4]{1,0:T(4,128)S(1)}, s32[4,4]{1,0:T(4,128)S(1)}, u32[]{:S(2)}, u32[]{:S(2)}) collective-permute-start(s32[4,4]{1,0:T(4,128)S(1)} %get-tuple-element.9), channel_id=1, source_target_pairs={{1,0},{2,1},{3,2},{4,3},{5,4},{6,5},{7,6},{8,7},{9,8},{10,9},{11,1... | collective-permute-start | bytes 200 | tf_op jit(solution)/shard_map/ppermute | solution.py:172
  160.4 13.3 %collective-permute-start = (s32[4,4]{1,0:T(4,128)S(1)}, s32[4,4]{1,0:T(4,128)S(1)}, u32[]{:S(2)}, u32[]{:S(2)}) collective-permute-start(s32[4,4]{1,0:T(4,128)S(1)} %get-tuple-element.10), channel_id=1, source_target_pairs={{0,1},{1,2},{2,3},{3,4},{4,5},{5,6},{6,7},{7,8},{8,9},{9,10},{10,1... | collective-permute-start | bytes 200 | tf_op jit(solution)/shard_map/ppermute | solution.py:171

commit v2 on v1

v2 whole, which is shorter than its diff:
```python
import jax
import jax.numpy as jnp
from jax import lax
from jax.experimental import pallas as pl
from jax.experimental.pallas import tpu as pltpu
from jax.sharding import PartitionSpec as P

AXES = ("row", "col")
BLOCK = 256
BAND = 4
LANES = (2 * BAND + 1) * BLOCK
BELOW = [(m, d) for m in range(1, BAND + 1) for d in range(m, BAND + 1)]
ABOVE = [(m, d) for m in range(BAND) for d in range(BAND - m)]

SCALARS = pl.BlockSpec(memory_space=pltpu.SMEM)
ANYWHERE = pl.BlockSpec(memory_space=pl.ANY)
ONCHIP = pl.BlockSpec(memory_space=pltpu.VMEM)


def partial_tiles(rows):
    return [
        (i, e) for i in range(rows) for e in range(BAND + 1) if i + e < BAND or i + e >= rows
    ]


def times_transposed(left, right):
    return lax.dot_general(
        left, right, (((1,), (1,)), ((), ())), preferred_element_type=jnp.float32
    )


def symmetric(raw):
    both = raw.astype(jnp.float32) + raw.T.astype(jnp.float32)
    return (0.5 * both).astype(jnp.bfloat16)


def limit(mebibytes):
    return pltpu.CompilerParams(vmem_limit_bytes=mebibytes << 20)


def onchip(array):
    return pltpu.with_memory_space_constraint(array, pltpu.VMEM)


def halo_kernel(kept, tiles, to_next, to_last, sem):
    rows = tiles.shape[1]
    copies = []
    start = 0
    for m in range(1, BAND + 1):
        count = BAND + 1 - m
        copies.append(
            (tiles.at[:, rows - m, pl.ds(m, count)], to_next.at[:, pl.ds(start, count)])
        )
        start += count
    start = 0
    for m in range(BAND):
        count = BAND - m
        copies.append((tiles.at[:, m, pl.ds(0, count)], to_last.at[:, pl.ds(start, count)]))
        start += count
    started = [
        pltpu.make_async_copy(source, target, sem.at[n])
        for n, (source, target) in enumerate(copies)
    ]
    for copy in started:
        copy.start()
    for copy in started:
        copy.wait()

    def mask(row, d, target, slot):
        if d > 0:

            @pl.when(kept[row, d - 1] == 0)
            def _():
                target[:, slot] = jnp.zeros_like(target[:, slot])

    for slot, (m, d) in enumerate(BELOW):
        mask(rows - m, d, to_next, slot)
    for slot, (m, d) in enumerate(ABOVE):
        mask(m, d, to_last, slot)


def halo_tiles(kept, tiles):
    parts, _, _, height, width = tiles.shape
    shape = pltpu.VMEM((parts, len(BELOW), height, width), tiles.dtype)
    return pl.pallas_call(
        halo_kernel,
        out_shape=(shape, shape),
        in_specs=[SCALARS, ANYWHERE],
        out_specs=(ONCHIP, ONCHIP),
        scratch_shapes=[pltpu.SemaphoreType.DMA((2 * BAND,))],
        compiler_params=limit(4),
    )(kept, tiles)


def local_kernel(kept, tiles, out, partial, strips, done, sem, out_sem):
    parts, rows, _, height, _ = tiles.shape
    waiting = partial_tiles(rows)

    def block(row, d):
        return strips.at[row, :, :, pl.ds((BAND + d) * BLOCK, BLOCK)]

    def load(row, d):
        return pltpu.make_async_copy(tiles.at[:, row, d], block(row, d), sem.at[row, d])

    def get(row, d):
        return block(row, d)[...].reshape(BLOCK, BLOCK)

    def put(row, d, value):
        block(row, d)[...] = value.reshape(parts, height, BLOCK)

    def store(i, e):
        return pltpu.make_async_copy(done.at[i, e], out.at[:, i, e], out_sem)

    for row in range(rows):
        for d in range(BAND + 1):
            load(row, d).start()

    def arrive(row):
        for d in range(BAND + 1):
            load(row, d).wait()
            if d > 0:

                @pl.when(kept[row, d - 1] == 0)
                def _():
                    put(row, d, jnp.zeros((BLOCK, BLOCK), jnp.bfloat16))

    def prepare(j):
        if j < rows:
            arrive(j)
            put(j, 0, symmetric(get(j, 0)))
        for m in range(1, BAND + 1):
            if 0 <= j - m < rows:
                put(j, -m, get(j - m, m).T)

    for j in range(BAND):
        prepare(j)
    for i in range(rows):
        prepare(i + BAND)
        for e in range(BAND + 1):
            j = i + e
            first = max(0, j - BAND)
            last = i + BAND if j < rows else rows - 1
            depth = (last + 1 - first) * BLOCK
            left = strips[i, :, :, pl.ds((first - i + BAND) * BLOCK, depth)]
            right = strips[j, :, :, pl.ds((first - j + BAND) * BLOCK, depth)]
            summed = times_transposed(left.reshape(BLOCK, depth), right.reshape(BLOCK, depth))
            if (i, e) in waiting:
                partial[waiting.index((i, e))] = summed
            else:
                if e > 0:
                    summed = jnp.where(kept[i, e - 1] != 0, summed, 0.0)
                done[i, e] = summed.astype(jnp.bfloat16).reshape(parts, height, BLOCK)
                store(i, e).start()
    for i in range(rows):
        for e in range(BAND + 1):
            if (i, e) not in waiting:
                store(i, e).wait()


def square_local(kept, tiles):
    parts, rows, width, height, _ = tiles.shape
    count = len(partial_tiles(rows))
    return pl.pallas_call(
        local_kernel,
        out_shape=(
            jax.ShapeDtypeStruct(tiles.shape, jnp.bfloat16),
            pltpu.VMEM((count, BLOCK, BLOCK), jnp.float32),
        ),
        in_specs=[SCALARS, ANYWHERE],
        out_specs=(ANYWHERE, ONCHIP),
        scratch_shapes=[
            pltpu.VMEM((rows + BAND, parts, height, LANES), jnp.bfloat16),
            pltpu.VMEM((rows, width, parts, height, BLOCK), jnp.bfloat16),
            pltpu.SemaphoreType.DMA((rows, width)),
            pltpu.SemaphoreType.DMA,
        ],
        compiler_params=limit(30),
    )(kept, tiles)


def border_kernel(kept, to_next, below, above, partial, _, out, done, out_sem):
    parts, rows, _, height, _ = out.shape
    waiting = partial_tiles(rows)

    def get(ref, slot):
        return ref[:, slot].reshape(BLOCK, BLOCK)

    def store(slot):
        i, e = waiting[slot]
        return pltpu.make_async_copy(done.at[slot], out.at[:, i, e], out_sem)

    def finish(i, e, summed):
        slot = waiting.index((i, e))
        summed = partial[slot] + summed
        if e > 0:
            summed = jnp.where(kept[i, e - 1] != 0, summed, 0.0)
        done[slot] = summed.astype(jnp.bfloat16).reshape(parts, height, BLOCK)
        store(slot).start()

    lower = {
        j: jnp.concatenate(
            [get(below, BELOW.index((m, j + m))).T for m in range(BAND - j, 0, -1)], axis=1
        )
        for j in range(BAND)
    }
    for j in range(BAND):
        depth = (BAND - j) * BLOCK
        for i in range(j + 1):
            left = lower[i][:, lower[i].shape[1] - depth :]
            finish(i, j - i, times_transposed(left, lower[j]))

    def corner(a, b):
        if a == b:
            return symmetric(get(above, ABOVE.index((a, 0))))
        if a < b:
            return get(above, ABOVE.index((a, b - a)))
        return get(above, ABOVE.index((b, a - b))).T

    square = [
        jnp.concatenate([corner(a, b) for b in range(BAND)], axis=1) for a in range(BAND)
    ]
    for i in range(rows - BAND, rows):
        reach = i + BAND + 1 - rows
        left = jnp.concatenate(
            [get(to_next, BELOW.index((rows - i, rows + b - i))) for b in range(reach)], axis=1
        )
        for a in range(reach):
            finish(i, rows + a - i, times_transposed(left, square[a][:, : reach * BLOCK]))
    for slot in range(len(waiting)):
        store(slot).wait()


def square_border(kept, to_next, below, above, partial, product):
    parts, rows, _, height, _ = product.shape
    return pl.pallas_call(
        border_kernel,
        out_shape=jax.ShapeDtypeStruct(product.shape, product.dtype),
        in_specs=[SCALARS, ONCHIP, ONCHIP, ONCHIP, ONCHIP, ANYWHERE],
        out_specs=ANYWHERE,
        scratch_shapes=[
            pltpu.VMEM((partial.shape[0], parts, height, BLOCK), jnp.bfloat16),
            pltpu.SemaphoreType.DMA,
        ],
        input_output_aliases={5: 0},
        compiler_params=limit(20),
    )(kept, *(onchip(a) for a in (to_next, below, above, partial)), product)


def shards(upper_tiles, occupied):
    parts = lax.axis_size("col")
    count = lax.axis_size("row") * parts
    rows, band = occupied.shape
    position = lax.axis_index("row") * parts + lax.axis_index("col")
    index = position * rows + jnp.arange(rows, dtype=jnp.int32)
    offsets = jnp.arange(1, band + 1, dtype=jnp.int32)
    inside = index[:, None] + offsets[None, :] < rows * count
    kept = ((occupied == 1) & inside).astype(jnp.int32)
    tiles = upper_tiles.reshape((parts, rows) + upper_tiles.shape[1:])
    tiles = lax.all_to_all(tiles, "col", 0, 0, tiled=True)
    to_next, to_last = halo_tiles(kept, tiles)
    below = lax.ppermute(to_next, AXES, [(p, p + 1) for p in range(count - 1)])
    above = lax.ppermute(to_last, AXES, [(p + 1, p) for p in range(count - 1)])
    product, partial = square_local(kept, tiles)
    product = square_border(kept, to_next, below, above, partial, product)
    product = lax.all_to_all(product, "col", 0, 0, tiled=True)
    return product.reshape(upper_tiles.shape)


def solution(mesh):
    return jax.shard_map(
        shards,
        mesh=mesh,
        in_specs=(P("row", None, "col", None), P(("row", "col"), None)),
        out_specs=P("row", None, "col", None),
        check_vma=False,
    )
```

time: 266 us -> 186 us (0.70)
  blocking collectives: 142 us -> 71.2 us
  Pallas kernels: 98.1 us -> 29.9 us
  waiting for transfers between devices: 10.9 us -> 70.2 us
    all_to_all x0 -> x1, waiting for transfers between devices: none -> 70.2 us  [shards(): tiles = lax.all_to_all(tiles, 'col', 0, 0, tiled=True)]
    all_to_all x1 -> x0, blocking collectives: 70 us -> none  [shards(): tiles = lax.all_to_all(tiles, 'col', 0, 0, tiled=True)]
    pallas_call x2 -> x3, Pallas kernels: 98.1 us -> 29.9 us  [the longest x1 19.3 us: square_local(): pl.pallas_call(local_kernel, out_shape=(jax.ShapeDtypeStruct(tiles.shape,...]
    ppermute x4 -> x2, waiting for transfers between devices: 10.9 us -> 0.01 us  [the longest x1 0.01 us: shards(): above = lax.ppermute(to_last, AXES, [(p + 1, p) for p in range(count - 1)])]
    ppermute x4 -> x2, starting transfers between devices: 12 us -> 4.43 us  [the longest x1 2.51 us: shards(): above = lax.ppermute(to_last, AXES, [(p + 1, p) for p in range(count - 1)])]
    all_to_all x0 -> x1, starting transfers between devices: none -> 7.16 us  [shards(): tiles = lax.all_to_all(tiles, 'col', 0, 0, tiled=True)]
  transfers between devices with their start and end apart: 4 -> 3, of which waited for: 1 -> 1; matrix products, arithmetic and copies ran while one was open for 0% -> 0% of each run, Pallas kernels for 0% -> 10%
where the time goes in v2:
time: 186 us
  blocking collectives  71.2 us (38%)
  waiting for transfers between devices  70.2 us (38%)
  Pallas kernels  29.9 us (16%)
  starting transfers between devices  11.6 us (6%)
  local copies, waits for them, and re-layouts  2.44 us (1%)
    all_to_all x1, blocking collectives, shards(): product = lax.all_to_all(product, 'col', 0, 0, tiled=True)  71.2 us
    all_to_all x1, waiting for transfers between devices, shards(): tiles = lax.all_to_all(tiles, 'col', 0, 0, tiled=True)  70.2 us
    pallas_call x1, Pallas kernels, square_local(): pl.pallas_call(local_kernel, out_shape=(jax.ShapeDtypeStruct(tiles.shape,...  19.3 us
    pallas_call x1, Pallas kernels, square_border(): pl.pallas_call(border_kernel, out_shape=jax.ShapeDtypeStruct(product.shap...  8.13 us
    all_to_all x1, starting transfers between devices, shards(): tiles = lax.all_to_all(tiles, 'col', 0, 0, tiled=True)  7.16 us
  transfers between devices with their start and end apart: 3, of which 1 were waited for; matrix products, arithmetic and copies ran while one was open for 0% of the time, Pallas kernels for 10%

profile of v2, /device:TPU:34, one launch (start us, length us, event | category | flops | bytes accessed | tf_op | source)
XLA Modules:
  0.0 185.5 jit_solution(7904584666433699582)
XLA Ops:
  0.0 0.0 copy-start
  0.0 7.2 %all-to-all-start = ((bf16[16,8,5,16,256]{4,3,2,1,0:T(8,128)(2,1)}), bf16[16,8,5,16,256]{4,3,2,1,0:T(8,128)(2,1)}, u32[]{:S(2)}, u32[]{:S(2)}) async-start(bf16[16,8,5,16,256]{4,3,2,1,0:T(8,128)(2,1)} %bitcast.3), calls=%async_computation | async-start | bytes 10485760 | tf_op jit(solution)/shard_map/all_to_all | solution.py:259
  7.2 0.0 copy-done
  7.2 0.1 copy.4
  7.3 0.1 fusion.1.kept
  7.4 70.2 %all-to-all-done.tiles = bf16[16,8,5,16,256]{4,3,2,1,0:T(8,128)(2,1)} async-done(((bf16[16,8,5,16,256]{4,3,2,1,0:T(8,128)(2,1)}), bf16[16,8,5,16,256]{4,3,2,1,0:T(8,128)(2,1)}, u32[]{:S(2)}, u32[]{:S(2)}) %all-to-all-start) | async-done | bytes 5242912 | tf_op jit(solution)/shard_map/all_to_all | solution.py:259
  77.6 2.5 %shard_map.28 = (bf16[16,10,16,256]{3,2,1,0:T(8,128)(2,1)S(1)}, bf16[16,10,16,256]{3,2,1,0:T(8,128)(2,1)S(1)}) custom-call(s32[8,4]{1,0:T(8,128)S(1)} %fusion.1.kept, bf16[16,8,5,16,256]{4,3,2,1,0:T(8,128)(2,1)} %all-to-all-done.tiles), custom_call_target="tpu_custom_call" | custom-call | tf_op jit(solution)/shard_map/pallas_call | solution.py:85
  80.0 2.5 %collective-permute-start.1 = (bf16[16,10,16,256]{3,2,1,0:T(8,128)(2,1)S(1)}, bf16[16,10,16,256]{3,2,1,0:T(8,128)(2,1)S(1)}, u32[]{:S(2)}, u32[]{:S(2)}) collective-permute-start(bf16[16,10,16,256]{3,2,1,0:T(8,128)(2,1)S(1)} %get-tuple-element.10), channel_id=1, source_target_pairs={{1,0},{2,1},{3,2},{4,3},{5,4},{6,5},{7,6},{8,7},{9,8},{10,9},{11,1... | collective-permute-start | bytes 3932168 | tf_op jit(solution)/shard_map/ppermute | solution.py:262
  82.6 1.9 %collective-permute-start = (bf16[16,10,16,256]{3,2,1,0:T(8,128)(2,1)S(1)}, bf16[16,10,16,256]{3,2,1,0:T(8,128)(2,1)S(1)}, u32[]{:S(2)}, u32[]{:S(2)}) collective-permute-start(bf16[16,10,16,256]{3,2,1,0:T(8,128)(2,1)S(1)} %get-tuple-element.9.to_next), channel_id=1, source_target_pairs={{0,1},{1,2},{2,3},{3,4},{4,5},{5,6},{6,7},{7,8},{8,9},{9,10},{10,1... | collective-permute-start | bytes 3932168 | tf_op jit(solution)/shard_map/ppermute | solution.py:261
  84.5 19.3 %shard_map.29 = (bf16[16,8,5,16,256]{4,3,2,1,0:T(8,128)(2,1)S(1)}, f32[20,256,256]{2,1,0:T(8,128)S(1)}) custom-call(s32[8,4]{1,0:T(8,128)S(1)} %fusion.1.kept, bf16[16,8,5,16,256]{4,3,2,1,0:T(8,128)(2,1)} %all-to-all-done.tiles), custom_call_target="tpu_custom_call" | custom-call | tf_op jit(solution)/shard_map/pallas_call | solution.py:163
  103.8 0.0 collective-permute-done.1.above
  103.8 0.0 collective-permute-done.below
  103.9 8.1 %shard_map.30 = bf16[16,8,5,16,256]{4,3,2,1,0:T(8,128)(2,1)S(1)} custom-call(s32[8,4]{1,0:T(8,128)S(1)} %fusion.1.kept, bf16[16,10,16,256]{3,2,1,0:T(8,128)(2,1)S(1)} %get-tuple-element.9.to_next, bf16[16,10,16,256]{3,2,1,0:T(8,128)(2,1)S(1)} %collective-permute-done.below, ...), custom_call_target="tpu_custom_call", output_to_operand_aliasing={{}: (5, {})} | custom-call | tf_op jit(solution)/shard_map/pallas_call | solution.py:235
  112.0 71.2 %all_to_all.10 = bf16[16,8,5,16,256]{4,3,2,1,0:T(8,128)(2,1)S(1)} all-to-all(bf16[16,8,5,16,256]{4,3,2,1,0:T(8,128)(2,1)S(1)} %shard_map.30), channel_id=1, replica_groups=mesh['row'=8,'col'=16] {'col'}, dimensions={0} | all-to-all | bytes 10485760 | tf_op jit(solution)/shard_map/all_to_all | solution.py:265
  183.2 2.4 %copy.7 = bf16[128,5,16,256]{3,2,1,0:T(8,128)(2,1)} copy(bf16[128,5,16,256]{3,2,1,0:T(8,128)(2,1)S(1)} %bitcast.2) | data formatting | bytes 10485760
  (2 shorter events, 0.0 us)
Async XLA Ops:
  0.0 7.2 %copy-start = (s32[8,4]{0,1:T(4,128)S(1)}, s32[8,4]{0,1:T(4,128)}, u32[]{:S(2)}) copy-start(s32[8,4]{0,1:T(4,128)} %param.3) | copy-start | bytes 388
  0.0 77.6 %all-to-all-start = ((bf16[16,8,5,16,256]{4,3,2,1,0:T(8,128)(2,1)}), bf16[16,8,5,16,256]{4,3,2,1,0:T(8,128)(2,1)}, u32[]{:S(2)}, u32[]{:S(2)}) async-start(bf16[16,8,5,16,256]{4,3,2,1,0:T(8,128)(2,1)} %bitcast.3), calls=%async_computation | async-start | bytes 10485760 | tf_op jit(solution)/shard_map/all_to_all | solution.py:259
  80.0 23.8 %collective-permute-start.1 = (bf16[16,10,16,256]{3,2,1,0:T(8,128)(2,1)S(1)}, bf16[16,10,16,256]{3,2,1,0:T(8,128)(2,1)S(1)}, u32[]{:S(2)}, u32[]{:S(2)}) collective-permute-start(bf16[16,10,16,256]{3,2,1,0:T(8,128)(2,1)S(1)} %get-tuple-element.10), channel_id=1, source_target_pairs={{1,0},{2,1},{3,2},{4,3},{5,4},{6,5},{7,6},{8,7},{9,8},{10,9},{11,1... | collective-permute-start | bytes 3932168 | tf_op jit(solution)/shard_map/ppermute | solution.py:262
  82.6 21.3 %collective-permute-start = (bf16[16,10,16,256]{3,2,1,0:T(8,128)(2,1)S(1)}, bf16[16,10,16,256]{3,2,1,0:T(8,128)(2,1)S(1)}, u32[]{:S(2)}, u32[]{:S(2)}) collective-permute-start(bf16[16,10,16,256]{3,2,1,0:T(8,128)(2,1)S(1)} %get-tuple-element.9.to_next), channel_id=1, source_target_pairs={{0,1},{1,2},{2,3},{3,4},{4,5},{5,6},{6,7},{7,8},{8,9},{9,10},{10,1... | collective-permute-start | bytes 3932168 | tf_op jit(solution)/shard_map/ppermute | solution.py:261

commit v3 on v2

v3 whole, which is shorter than its diff:
```python
import jax
import jax.numpy as jnp
from jax import lax
from jax.experimental import pallas as pl
from jax.experimental.pallas import tpu as pltpu
from jax.sharding import PartitionSpec as P

AXES = ("row", "col")
BLOCK = 256
BAND = 4
LANES = (2 * BAND + 1) * BLOCK
BELOW = [(m, d) for m in range(1, BAND + 1) for d in range(m, BAND + 1)]
ABOVE = [(m, d) for m in range(BAND) for d in range(BAND - m)]

SCALARS = pl.BlockSpec(memory_space=pltpu.SMEM)
ANYWHERE = pl.BlockSpec(memory_space=pl.ANY)
ONCHIP = pl.BlockSpec(memory_space=pltpu.VMEM)


def partial_tiles(rows):
    return [
        (i, e) for i in range(rows) for e in range(BAND + 1) if i + e < BAND or i + e >= rows
    ]


def keep(occupied, row, d):
    rows = occupied.shape[0]
    here = lax.axis_index("row") * lax.axis_size("col") + lax.axis_index("col")
    there = lax.axis_size("row") * lax.axis_size("col")
    return (occupied[row, d - 1] == 1) & (here * rows + row + d < there * rows)


def times_transposed(left, right):
    return lax.dot_general(
        left, right, (((1,), (1,)), ((), ())), preferred_element_type=jnp.float32
    )


def symmetric(raw):
    both = raw.astype(jnp.float32) + raw.T.astype(jnp.float32)
    return (0.5 * both).astype(jnp.bfloat16)


def limit(mebibytes):
    return pltpu.CompilerParams(vmem_limit_bytes=mebibytes << 20)


def onchip(array):
    return pltpu.with_memory_space_constraint(array, pltpu.VMEM)


def halo_kernel(occupied, tiles, to_next, to_last, sem):
    rows = tiles.shape[1]
    copies = []
    start = 0
    for m in range(1, BAND + 1):
        count = BAND + 1 - m
        copies.append(
            (tiles.at[:, rows - m, pl.ds(m, count)], to_next.at[:, pl.ds(start, count)])
        )
        start += count
    start = 0
    for m in range(BAND):
        count = BAND - m
        copies.append((tiles.at[:, m, pl.ds(0, count)], to_last.at[:, pl.ds(start, count)]))
        start += count
    started = [
        pltpu.make_async_copy(source, target, sem.at[n])
        for n, (source, target) in enumerate(copies)
    ]
    for copy in started:
        copy.start()
    for copy in started:
        copy.wait()

    def mask(row, d, target, slot):
        if d > 0:

            @pl.when(jnp.logical_not(keep(occupied, row, d)))
            def _():
                target[:, slot] = jnp.zeros_like(target[:, slot])

    for slot, (m, d) in enumerate(BELOW):
        mask(rows - m, d, to_next, slot)
    for slot, (m, d) in enumerate(ABOVE):
        mask(m, d, to_last, slot)


def halo_tiles(occupied, tiles):
    parts, _, _, height, width = tiles.shape
    shape = pltpu.VMEM((parts, len(BELOW), height, width), tiles.dtype)
    return pl.pallas_call(
        halo_kernel,
        out_shape=(shape, shape),
        in_specs=[SCALARS, ANYWHERE],
        out_specs=(ONCHIP, ONCHIP),
        scratch_shapes=[pltpu.SemaphoreType.DMA((2 * BAND,))],
        compiler_params=limit(4),
    )(occupied, tiles)


def local_kernel(occupied, tiles, out, partial, strips, sem):
    parts, rows, _, height, _ = tiles.shape
    waiting = partial_tiles(rows)

    def block(row, d):
        return strips.at[row, :, :, pl.ds((BAND + d) * BLOCK, BLOCK)]

    def load(row, d):
        return pltpu.make_async_copy(tiles.at[:, row, d], block(row, d), sem.at[row, d])

    def get(row, d):
        return block(row, d)[...].reshape(BLOCK, BLOCK)

    def put(row, d, value):
        block(row, d)[...] = value.reshape(parts, height, BLOCK)

    for row in range(rows):
        for d in range(BAND + 1):
            load(row, d).start()

    def arrive(row):
        for d in range(BAND + 1):
            load(row, d).wait()
            if d > 0:

                @pl.when(jnp.logical_not(keep(occupied, row, d)))
                def _():
                    put(row, d, jnp.zeros((BLOCK, BLOCK), jnp.bfloat16))

    def prepare(j):
        if j < rows:
            arrive(j)
            put(j, 0, symmetric(get(j, 0)))
        for m in range(1, BAND + 1):
            if 0 <= j - m < rows:
                put(j, -m, get(j - m, m).T)

    for j in range(BAND):
        prepare(j)
    for i in range(rows):
        prepare(i + BAND)
        for e in range(BAND + 1):
            j = i + e
            first = max(0, j - BAND)
            last = i + BAND if j < rows else rows - 1
            depth = (last + 1 - first) * BLOCK
            rows_i = strips[i, :, :, pl.ds((first - i + BAND) * BLOCK, depth)]
            rows_j = strips[j, :, :, pl.ds((first - j + BAND) * BLOCK, depth)]
            summed = times_transposed(rows_i.reshape(BLOCK, depth), rows_j.reshape(BLOCK, depth))
            if (i, e) in waiting:
                partial[waiting.index((i, e))] = summed
            else:
                if e > 0:
                    summed = jnp.where(keep(occupied, i, e), summed, 0.0)
                out[:, i, e] = summed.astype(jnp.bfloat16).reshape(parts, height, BLOCK)


def square_local(occupied, tiles):
    parts, rows, width, height, _ = tiles.shape
    count = len(partial_tiles(rows))
    return pl.pallas_call(
        local_kernel,
        out_shape=(
            pltpu.VMEM(tiles.shape, jnp.bfloat16),
            pltpu.VMEM((count, BLOCK, BLOCK), jnp.float32),
        ),
        in_specs=[SCALARS, ANYWHERE],
        out_specs=(ONCHIP, ONCHIP),
        scratch_shapes=[
            pltpu.VMEM((rows + BAND, parts, height, LANES), jnp.bfloat16),
            pltpu.SemaphoreType.DMA((rows, width)),
        ],
        compiler_params=limit(30),
    )(occupied, tiles)


def border_kernel(occupied, to_next, below, above, partial, _, out):
    parts, rows, _, height, _ = out.shape
    waiting = partial_tiles(rows)

    def get(ref, slot):
        return ref[:, slot].reshape(BLOCK, BLOCK)

    def finish(i, e, summed):
        slot = waiting.index((i, e))
        summed = partial[slot] + summed
        if e > 0:
            summed = jnp.where(keep(occupied, i, e), summed, 0.0)
        out[:, i, e] = summed.astype(jnp.bfloat16).reshape(parts, height, BLOCK)

    lower = {
        j: jnp.concatenate(
            [get(below, BELOW.index((m, j + m))).T for m in range(BAND - j, 0, -1)], axis=1
        )
        for j in range(BAND)
    }
    for j in range(BAND):
        depth = (BAND - j) * BLOCK
        for i in range(j + 1):
            rows_i = lower[i][:, lower[i].shape[1] - depth :]
            finish(i, j - i, times_transposed(rows_i, lower[j]))

    def corner(a, b):
        if a == b:
            return symmetric(get(above, ABOVE.index((a, 0))))
        if a < b:
            return get(above, ABOVE.index((a, b - a)))
        return get(above, ABOVE.index((b, a - b))).T

    square = [
        jnp.concatenate([corner(a, b) for b in range(BAND)], axis=1) for a in range(BAND)
    ]
    for i in range(rows - BAND, rows):
        reach = i + BAND + 1 - rows
        rows_i = jnp.concatenate(
            [get(to_next, BELOW.index((rows - i, rows + b - i))) for b in range(reach)], axis=1
        )
        for a in range(reach):
            finish(i, rows + a - i, times_transposed(rows_i, square[a][:, : reach * BLOCK]))


def square_border(occupied, to_next, below, above, partial, product):
    return pl.pallas_call(
        border_kernel,
        out_shape=pltpu.VMEM(product.shape, product.dtype),
        in_specs=[SCALARS] + [ONCHIP] * 5,
        out_specs=ONCHIP,
        input_output_aliases={5: 0},
        compiler_params=limit(20),
    )(occupied, *(onchip(a) for a in (to_next, below, above, partial, product)))


def shards(upper_tiles, occupied):
    parts = lax.axis_size("col")
    count = lax.axis_size("row") * parts
    rows = occupied.shape[0]
    tiles = upper_tiles.reshape((parts, rows) + upper_tiles.shape[1:])
    tiles = lax.all_to_all(tiles, "col", 0, 0, tiled=True)
    tiles, occupied = lax.optimization_barrier((tiles, occupied))
    to_next, to_last = halo_tiles(occupied, tiles)
    below = lax.ppermute(to_next, AXES, [(p, p + 1) for p in range(count - 1)])
    above = lax.ppermute(to_last, AXES, [(p + 1, p) for p in range(count - 1)])
    product, partial = square_local(occupied, tiles)
    product = square_border(occupied, to_next, below, above, partial, product)
    product = lax.all_to_all(product, "col", 0, 0, tiled=True)
    return product.reshape(upper_tiles.shape)


def solution(mesh):
    return jax.shard_map(
        shards,
        mesh=mesh,
        in_specs=(P("row", None, "col", None), P(("row", "col"), None)),
        out_specs=P("row", None, "col", None),
        check_vma=False,
    )
```

time: 186 us -> 172 us (0.925)
  blocking collectives: 71.2 us -> 139 us
  waiting for transfers between devices: 70.2 us -> 7.11 us
  Pallas kernels: 29.9 us -> 15.3 us
  starting transfers between devices: 11.6 us -> 4.46 us
  local copies, waits for them, and re-layouts: 2.44 us -> 4.93 us
    all_to_all x1 -> x0, waiting for transfers between devices: 70.2 us -> none  [shards(): tiles = lax.all_to_all(tiles, 'col', 0, 0, tiled=True)]
    all_to_all x0 -> x1, blocking collectives: none -> 70.1 us  [shards(): tiles = lax.all_to_all(tiles, 'col', 0, 0, tiled=True)]
    pallas_call x2, Pallas kernels: 27.5 us -> 14.2 us  [the longest x1 11.5 us: square_local(): pl.pallas_call(local_kernel, out_shape=(pltpu.VMEM(tiles.shape, jnp.bfloa...]
    all_to_all x1 -> x0, starting transfers between devices: 7.16 us -> none  [shards(): tiles = lax.all_to_all(tiles, 'col', 0, 0, tiled=True)]
    ppermute x1, waiting for transfers between devices: 0.01 us -> 5.93 us  [shards(): below = lax.ppermute(to_next, AXES, [(p, p + 1) for p in range(count - 1)])]
    unnamed x4 -> x7, local copies, waits for them, and re-layouts: 2.44 us -> 4.85 us
    all_to_all x1, blocking collectives: 71.2 us -> 69.1 us  [shards(): product = lax.all_to_all(product, 'col', 0, 0, tiled=True)]
  transfers between devices with their start and end apart: 3 -> 2, of which waited for: 1 -> 2; matrix products, arithmetic and copies ran while one was open for 0% -> 0% of each run, Pallas kernels for 10% -> 7%
where the time goes in v3:
time: 172 us; the launch traced here: 171 us
  blocking collectives  139 us (81%)
  Pallas kernels  15.3 us (9%)
  waiting for transfers between devices  7.11 us (4%)
  local copies, waits for them, and re-layouts  4.93 us (3%)
  starting transfers between devices  4.46 us (3%)
    all_to_all x1, blocking collectives, shards(): tiles = lax.all_to_all(tiles, 'col', 0, 0, tiled=True)  70.1 us
    all_to_all x1, blocking collectives, shards(): product = lax.all_to_all(product, 'col', 0, 0, tiled=True)  69.1 us
    pallas_call x1, Pallas kernels, square_local(): pl.pallas_call(local_kernel, out_shape=(pltpu.VMEM(tiles.shape, jnp.bfloa...  11.5 us
    ppermute x1, waiting for transfers between devices, shards(): below = lax.ppermute(to_next, AXES, [(p, p + 1) for p in range(count - 1)])  5.93 us
    unnamed x7, local copies, waits for them, and re-layouts  4.85 us
  transfers between devices with their start and end apart: 2, of which 2 were waited for; matrix products, arithmetic and copies ran while one was open for 0% of the time, Pallas kernels for 7%

profile of v3, /device:TPU:34, one launch (start us, length us, event | category | flops | bytes accessed | tf_op | source)
XLA Modules:
  0.0 171.0 jit_solution(12884912527434539162)
XLA Ops:
  0.0 0.0 copy-start.2
  0.0 70.1 %all_to_all.10.tiles = bf16[16,8,5,16,256]{4,3,2,1,0:T(8,128)(2,1)} all-to-all(bf16[16,8,5,16,256]{4,3,2,1,0:T(8,128)(2,1)} %bitcast.3), channel_id=1, replica_groups=mesh['row'=8,'col'=16] {'col'}, dimensions={0} | all-to-all | bytes 10485760 | tf_op jit(solution)/shard_map/all_to_all | solution.py:239
  70.1 0.0 copy-done.2
  70.1 0.1 copy.6.occupied
  70.2 0.0 copy-start
  70.2 2.5 %copy-done = bf16[16,8,5,16,256]{4,3,2,1,0:T(8,128)(2,1)S(1)} copy-done((bf16[16,8,5,16,256]{4,3,2,1,0:T(8,128)(2,1)S(1)}, bf16[16,8,5,16,256]{4,3,2,1,0:T(8,128)(2,1)}, u32[]{:S(2)}) %copy-start) | copy-done | bytes 5242904
  72.7 0.0 copy-start.1
  72.7 1.1 shard_map.28
  73.8 2.1 %collective-permute-start.1 = (bf16[16,10,16,256]{3,2,1,0:T(8,128)(2,1)S(1)}, bf16[16,10,16,256]{3,2,1,0:T(8,128)(2,1)S(1)}, u32[]{:S(2)}, u32[]{:S(2)}) collective-permute-start(bf16[16,10,16,256]{3,2,1,0:T(8,128)(2,1)S(1)} %get-tuple-element.14), channel_id=1, source_target_pairs={{1,0},{2,1},{3,2},{4,3},{5,4},{6,5},{7,6},{8,7},{9,8},{10,9},{11,1... | collective-permute-start | bytes 3932168 | tf_op jit(solution)/shard_map/ppermute | solution.py:243
  75.9 2.4 %collective-permute-start = (bf16[16,10,16,256]{3,2,1,0:T(8,128)(2,1)S(1)}, bf16[16,10,16,256]{3,2,1,0:T(8,128)(2,1)S(1)}, u32[]{:S(2)}, u32[]{:S(2)}) collective-permute-start(bf16[16,10,16,256]{3,2,1,0:T(8,128)(2,1)S(1)} %get-tuple-element.13.to_next), channel_id=1, source_target_pairs={{0,1},{1,2},{2,3},{3,4},{4,5},{5,6},{6,7},{7,8},{8,9},{9,10},{10,1... | collective-permute-start | bytes 3932168 | tf_op jit(solution)/shard_map/ppermute | solution.py:242
  78.3 0.0 copy-done.1
  78.3 11.5 %shard_map.29 = (bf16[16,8,5,16,256]{4,3,2,1,0:T(8,128)(2,1)S(1)}, f32[20,256,256]{2,1,0:T(8,128)S(1)}) custom-call(s32[8,4]{1,0:T(8,128)S(1)} %copy.6.occupied, bf16[16,8,5,16,256]{4,3,2,1,0:T(8,128)(2,1)S(1)} %copy-done.1), custom_call_target="tpu_custom_call" | custom-call | tf_op jit(solution)/shard_map/pallas_call | solution.py:162
  89.8 1.2 collective-permute-done.1.above
  91.0 5.9 %collective-permute-done.below = bf16[16,10,16,256]{3,2,1,0:T(8,128)(2,1)S(1)} collective-permute-done((bf16[16,10,16,256]{3,2,1,0:T(8,128)(2,1)S(1)}, bf16[16,10,16,256]{3,2,1,0:T(8,128)(2,1)S(1)}, u32[]{:S(2)}, u32[]{:S(2)}) %collective-permute-start) | collective-permute-done | bytes 1310752 | tf_op jit(solution)/shard_map/ppermute | solution.py:242
  96.9 2.7 %shard_map.30 = bf16[16,8,5,16,256]{4,3,2,1,0:T(8,128)(2,1)S(1)} custom-call(s32[8,4]{1,0:T(8,128)S(1)} %copy.6.occupied, bf16[16,10,16,256]{3,2,1,0:T(8,128)(2,1)S(1)} %get-tuple-element.13.to_next, bf16[16,10,16,256]{3,2,1,0:T(8,128)(2,1)S(1)} %collective-permute-done.below, ...), custom_call_target="tpu_custom_call", output_to_operand_aliasing={{}: (5, {})} | custom-call | tf_op jit(solution)/shard_map/pallas_call | solution.py:224
  99.6 69.1 %all_to_all.11 = bf16[16,8,5,16,256]{4,3,2,1,0:T(8,128)(2,1)S(1)} all-to-all(bf16[16,8,5,16,256]{4,3,2,1,0:T(8,128)(2,1)S(1)} %shard_map.30), channel_id=1, replica_groups=mesh['row'=8,'col'=16] {'col'}, dimensions={0} | all-to-all | bytes 10485760 | tf_op jit(solution)/shard_map/all_to_all | solution.py:246
  168.7 2.4 %copy.9 = bf16[128,5,16,256]{3,2,1,0:T(8,128)(2,1)} copy(bf16[128,5,16,256]{3,2,1,0:T(8,128)(2,1)S(1)} %bitcast.2) | data formatting | bytes 10485760
Async XLA Ops:
  0.0 70.1 %copy-start.2 = (s32[8,4]{0,1:T(4,128)S(1)}, s32[8,4]{0,1:T(4,128)}, u32[]{:S(2)}) copy-start(s32[8,4]{0,1:T(4,128)} %param.3) | copy-start | bytes 388
  70.2 2.5 %copy-start = (bf16[16,8,5,16,256]{4,3,2,1,0:T(8,128)(2,1)S(1)}, bf16[16,8,5,16,256]{4,3,2,1,0:T(8,128)(2,1)}, u32[]{:S(2)}) copy-start(bf16[16,8,5,16,256]{4,3,2,1,0:T(8,128)(2,1)} %all_to_all.10.tiles) | copy-start | bytes 15728644
  72.7 5.6 %copy-start.1 = (bf16[16,8,5,16,256]{4,3,2,1,0:T(8,128)(2,1)S(1)}, bf16[16,8,5,16,256]{4,3,2,1,0:T(8,128)(2,1)}, u32[]{:S(2)}) copy-start(bf16[16,8,5,16,256]{4,3,2,1,0:T(8,128)(2,1)} %all_to_all.10.tiles) | copy-start | bytes 15728644
  73.8 17.2 %collective-permute-start.1 = (bf16[16,10,16,256]{3,2,1,0:T(8,128)(2,1)S(1)}, bf16[16,10,16,256]{3,2,1,0:T(8,128)(2,1)S(1)}, u32[]{:S(2)}, u32[]{:S(2)}) collective-permute-start(bf16[16,10,16,256]{3,2,1,0:T(8,128)(2,1)S(1)} %get-tuple-element.14), channel_id=1, source_target_pairs={{1,0},{2,1},{3,2},{4,3},{5,4},{6,5},{7,6},{8,7},{9,8},{10,9},{11,1... | collective-permute-start | bytes 3932168 | tf_op jit(solution)/shard_map/ppermute | solution.py:243
  75.9 21.0 %collective-permute-start = (bf16[16,10,16,256]{3,2,1,0:T(8,128)(2,1)S(1)}, bf16[16,10,16,256]{3,2,1,0:T(8,128)(2,1)S(1)}, u32[]{:S(2)}, u32[]{:S(2)}) collective-permute-start(bf16[16,10,16,256]{3,2,1,0:T(8,128)(2,1)S(1)} %get-tuple-element.13.to_next), channel_id=1, source_target_pairs={{0,1},{1,2},{2,3},{3,4},{4,5},{5,6},{6,7},{7,8},{8,9},{9,10},{10,1... | collective-permute-start | bytes 3932168 | tf_op jit(solution)/shard_map/ppermute | solution.py:242

commit v4 on v3

--- a/solution.py
+++ b/solution.py
@@ -13,7 +13,7 @@
 ABOVE = [(m, d) for m in range(BAND) for d in range(BAND - m)]
 
 SCALARS = pl.BlockSpec(memory_space=pltpu.SMEM)
-ANYWHERE = pl.BlockSpec(memory_space=pl.ANY)
+OFFCHIP = pl.BlockSpec(memory_space=pltpu.HBM)
 ONCHIP = pl.BlockSpec(memory_space=pltpu.VMEM)
 
 
@@ -49,41 +49,42 @@
     return pltpu.with_memory_space_constraint(array, pltpu.VMEM)
 
 
-def halo_kernel(occupied, tiles, to_next, to_last, sem):
+def is_odd():
+    return lax.rem(lax.axis_index("col"), 2)
+
+
+def halo_kernel(occupied, tiles, across, beside, sem):
     rows = tiles.shape[1]
+    odd = is_odd()
     copies = []
+    spans = []
     start = 0
     for m in range(1, BAND + 1):
         count = BAND + 1 - m
-        copies.append(
-            (tiles.at[:, rows - m, pl.ds(m, count)], to_next.at[:, pl.ds(start, count)])
-        )
+        for target, upward in ((across, odd), (beside, 1 - odd)):
+            row = upward * (rows - m) + (1 - upward) * (m - 1)
+            first = upward * m
+            copies.append(
+                pltpu.make_async_copy(
+                    tiles.at[:, row, pl.ds(first, count)],
+                    target.at[:, pl.ds(start, count)],
+                    sem.at[len(copies)],
+                )
+            )
+            spans.append((target, start, count, row, first))
         start += count
-    start = 0
-    for m in range(BAND):
-        count = BAND - m
-        copies.append((tiles.at[:, m, pl.ds(0, count)], to_last.at[:, pl.ds(start, count)]))
-        start += count
-    started = [
-        pltpu.make_async_copy(source, target, sem.at[n])
-        for n, (source, target) in enumerate(copies)
-    ]
-    for copy in started:
+    for copy in copies:
         copy.start()
-    for copy in started:
+    for copy in copies:
         copy.wait()
-
-    def mask(row, d, target, slot):
-        if d > 0:
-
-            @pl.when(jnp.logical_not(keep(occupied, row, d)))
+    for target, start, count, row, first in spans:
+        for step in range(count):
+            d = first + step
+            dropped = (d > 0) & jnp.logical_not(keep(occupied, row, jnp.maximum(d, 1)))
+
+            @pl.when(dropped)
             def _():
-                target[:, slot] = jnp.zeros_like(target[:, slot])
-
-    for slot, (m, d) in enumerate(BELOW):
-        mask(rows - m, d, to_next, slot)
-    for slot, (m, d) in enumerate(ABOVE):
-        mask(m, d, to_last, slot)
+                target[:, start + step] = jnp.zeros_like(target[:, start + step])
 
 
 def halo_tiles(occupied, tiles):
@@ -92,11 +93,11 @@
     return pl.pallas_call(
         halo_kernel,
         out_shape=(shape, shape),
-        in_specs=[SCALARS, ANYWHERE],
+        in_specs=[SCALARS, OFFCHIP],
         out_specs=(ONCHIP, ONCHIP),
         scratch_shapes=[pltpu.SemaphoreType.DMA((2 * BAND,))],
         compiler_params=limit(4),
-    )(occupied, tiles)
+    )(occupied, pltpu.with_memory_space_constraint(tiles, pltpu.HBM))
 
 
 def local_kernel(occupied, tiles, out, partial, strips, sem):
@@ -165,22 +166,26 @@
             pltpu.VMEM(tiles.shape, jnp.bfloat16),
             pltpu.VMEM((count, BLOCK, BLOCK), jnp.float32),
         ),
-        in_specs=[SCALARS, ANYWHERE],
+        in_specs=[SCALARS, OFFCHIP],
         out_specs=(ONCHIP, ONCHIP),
         scratch_shapes=[
             pltpu.VMEM((rows + BAND, parts, height, LANES), jnp.bfloat16),
             pltpu.SemaphoreType.DMA((rows, width)),
         ],
         compiler_params=limit(30),
-    )(occupied, tiles)
-
-
-def border_kernel(occupied, to_next, below, above, partial, _, out):
+    )(occupied, pltpu.with_memory_space_constraint(tiles, pltpu.HBM))
+
+
+def border_kernel(occupied, sent_across, sent_beside, across, beside, partial, _, out):
+    odd = is_odd() == 1
+    to_next = (sent_across, sent_beside)
+    below = (beside, across)
+    above = (across, beside)
     parts, rows, _, height, _ = out.shape
     waiting = partial_tiles(rows)
 
-    def get(ref, slot):
-        return ref[:, slot].reshape(BLOCK, BLOCK)
+    def get(refs, slot):
+        return jnp.where(odd, refs[0][:, slot], refs[1][:, slot]).reshape(BLOCK, BLOCK)
 
     def finish(i, e, summed):
         slot = waiting.index((i, e))
@@ -220,15 +225,19 @@
             finish(i, rows + a - i, times_transposed(rows_i, square[a][:, : reach * BLOCK]))
 
 
-def square_border(occupied, to_next, below, above, partial, product):
+def square_border(occupied, halo, partial, product):
     return pl.pallas_call(
         border_kernel,
         out_shape=pltpu.VMEM(product.shape, product.dtype),
-        in_specs=[SCALARS] + [ONCHIP] * 5,
+        in_specs=[SCALARS] + [ONCHIP] * 6,
         out_specs=ONCHIP,
-        input_output_aliases={5: 0},
+        input_output_aliases={6: 0},
         compiler_params=limit(20),
-    )(occupied, *(onchip(a) for a in (to_next, below, above, partial, product)))
+    )(occupied, *(onchip(a) for a in (*halo, partial, product)))
+
+
+def swaps(firsts):
+    return [pair for p in firsts for pair in ((p, p + 1), (p + 1, p))]
 
 
 def shards(upper_tiles, occupied):
@@ -238,11 +247,12 @@
     tiles = upper_tiles.reshape((parts, rows) + upper_tiles.shape[1:])
     tiles = lax.all_to_all(tiles, "col", 0, 0, tiled=True)
     tiles, occupied = lax.optimization_barrier((tiles, occupied))
-    to_next, to_last = halo_tiles(occupied, tiles)
-    below = lax.ppermute(to_next, AXES, [(p, p + 1) for p in range(count - 1)])
-    above = lax.ppermute(to_last, AXES, [(p + 1, p) for p in range(count - 1)])
+    sent_across, sent_beside = halo_tiles(occupied, tiles)
+    across = lax.ppermute(sent_across, AXES, swaps(range(1, count - 1, 2)))
+    beside = lax.ppermute(sent_beside, AXES, swaps(range(0, count, 2)))
     product, partial = square_local(occupied, tiles)
-    product = square_border(occupied, to_next, below, above, partial, product)
+    halo = (sent_across, sent_beside, across, beside)
+    product = square_border(occupied, halo, partial, product)
     product = lax.all_to_all(product, "col", 0, 0, tiled=True)
     return product.reshape(upper_tiles.shape)
 

time: 172 us -> 168 us (0.977)
  Pallas kernels: 15.3 us -> 17.9 us
  local copies, waits for them, and re-layouts: 4.93 us -> 2.44 us
  starting transfers between devices: 4.46 us -> 2.01 us
  blocking collectives: 139 us -> 137 us
    unnamed x7 -> x3, local copies, waits for them, and re-layouts: 4.85 us -> 2.36 us
    ppermute x2, starting transfers between devices: 4.46 us -> 2.01 us  [the longest x1 1.92 us: shards(): across = lax.ppermute(sent_across, AXES, swaps(range(1, count - 1, 2)))]
    all_to_all x1, blocking collectives: 69.1 us -> 66.6 us  [shards(): product = lax.all_to_all(product, 'col', 0, 0, tiled=True)]
  transfers between devices with their start and end apart: 2 -> 2, of which waited for: 2 -> 1; matrix products, arithmetic and copies ran while one was open for 0% -> 0% of each run, Pallas kernels for 7% -> 7%
where the time goes in v4:
time: 168 us; the launch traced here: 166 us
  blocking collectives  137 us (82%)
  Pallas kernels  17.9 us (11%)
  waiting for transfers between devices  6.66 us (4%)
  local copies, waits for them, and re-layouts  2.44 us (1%)
  starting transfers between devices  2.01 us (1%)
    all_to_all x1, blocking collectives, shards(): tiles = lax.all_to_all(tiles, 'col', 0, 0, tiled=True)  70.1 us
    all_to_all x1, blocking collectives, shards(): product = lax.all_to_all(product, 'col', 0, 0, tiled=True)  66.6 us
    pallas_call x1, Pallas kernels, square_local(): pl.pallas_call(local_kernel, out_shape=(pltpu.VMEM(tiles.shape, jnp.bfloa...  12.3 us
    ppermute x1, waiting for transfers between devices, shards(): across = lax.ppermute(sent_across, AXES, swaps(range(1, count - 1, 2)))  6.66 us
  transfers between devices with their start and end apart: 2, of which 1 were waited for; matrix products, arithmetic and copies ran while one was open for 0% of the time, Pallas kernels for 7%

profile of v4, /device:TPU:34, one launch (start us, length us, event | category | flops | bytes accessed | tf_op | source)
XLA Modules:
  0.0 165.8 jit_solution(1241826332706668590)
XLA Ops:
  0.0 0.0 copy-start
  0.0 70.1 %all_to_all.10.tiles = bf16[16,8,5,16,256]{4,3,2,1,0:T(8,128)(2,1)} all-to-all(bf16[16,8,5,16,256]{4,3,2,1,0:T(8,128)(2,1)} %bitcast.3), channel_id=1, replica_groups=mesh['row'=8,'col'=16] {'col'}, dimensions={0} | all-to-all | bytes 10485760 | tf_op jit(solution)/shard_map/all_to_all | solution.py:248
  70.1 0.0 copy-done
  70.1 0.1 copy.6.occupied
  70.2 2.7 %shard_map.28 = (bf16[16,10,16,256]{3,2,1,0:T(8,128)(2,1)S(1)}, bf16[16,10,16,256]{3,2,1,0:T(8,128)(2,1)S(1)}) custom-call(s32[8,4]{1,0:T(8,128)S(1)} %copy.6.occupied, bf16[16,8,5,16,256]{4,3,2,1,0:T(8,128)(2,1)} %all_to_all.10.tiles), custom_call_target="tpu_custom_call" | custom-call | tf_op jit(solution)/shard_map/pallas_call | solution.py:93
  72.9 1.9 %collective-permute-start = (bf16[16,10,16,256]{3,2,1,0:T(8,128)(2,1)S(1)}, bf16[16,10,16,256]{3,2,1,0:T(8,128)(2,1)S(1)}, u32[]{:S(2)}, u32[]{:S(2)}) collective-permute-start(bf16[16,10,16,256]{3,2,1,0:T(8,128)(2,1)S(1)} %get-tuple-element.13.sent_across), channel_id=1, source_target_pairs={{1,2},{2,1},{3,4},{4,3},{5,6},{6,5},{7,8},{8,7},{9,10},{10,9},{11,... | collective-permute-start | bytes 3932168 | tf_op jit(solution)/shard_map/ppermute | solution.py:251
  74.8 0.1 collective-permute-start.1
  74.9 12.3 %shard_map.29 = (bf16[16,8,5,16,256]{4,3,2,1,0:T(8,128)(2,1)S(1)}, f32[20,256,256]{2,1,0:T(8,128)S(1)}) custom-call(s32[8,4]{1,0:T(8,128)S(1)} %copy.6.occupied, bf16[16,8,5,16,256]{4,3,2,1,0:T(8,128)(2,1)} %all_to_all.10.tiles), custom_call_target="tpu_custom_call" | custom-call | tf_op jit(solution)/shard_map/pallas_call | solution.py:163
  87.3 6.7 %collective-permute-done.across = bf16[16,10,16,256]{3,2,1,0:T(8,128)(2,1)S(1)} collective-permute-done((bf16[16,10,16,256]{3,2,1,0:T(8,128)(2,1)S(1)}, bf16[16,10,16,256]{3,2,1,0:T(8,128)(2,1)S(1)}, u32[]{:S(2)}, u32[]{:S(2)}) %collective-permute-start) | collective-permute-done | bytes 1310752 | tf_op jit(solution)/shard_map/ppermute | solution.py:251
  93.9 0.0 collective-permute-done.1.beside
  93.9 2.8 %shard_map.30 = bf16[16,8,5,16,256]{4,3,2,1,0:T(8,128)(2,1)S(1)} custom-call(s32[8,4]{1,0:T(8,128)S(1)} %copy.6.occupied, bf16[16,10,16,256]{3,2,1,0:T(8,128)(2,1)S(1)} %get-tuple-element.13.sent_across, bf16[16,10,16,256]{3,2,1,0:T(8,128)(2,1)S(1)} %get-tuple-element.14.sent_beside, ...), custom_call_target="tpu_custom_call", output_to_operand_aliasing={{}: (6, {})} | custom-call | tf_op jit(solution)/shard_map/pallas_call | solution.py:229
  96.8 66.6 %all_to_all.11 = bf16[16,8,5,16,256]{4,3,2,1,0:T(8,128)(2,1)S(1)} all-to-all(bf16[16,8,5,16,256]{4,3,2,1,0:T(8,128)(2,1)S(1)} %shard_map.30), channel_id=1, replica_groups=mesh['row'=8,'col'=16] {'col'}, dimensions={0} | all-to-all | bytes 10485760 | tf_op jit(solution)/shard_map/all_to_all | solution.py:256
  163.4 2.4 %copy.9 = bf16[128,5,16,256]{3,2,1,0:T(8,128)(2,1)} copy(bf16[128,5,16,256]{3,2,1,0:T(8,128)(2,1)S(1)} %bitcast.2) | data formatting | bytes 10485760
Async XLA Ops:
  0.0 70.1 %copy-start = (s32[8,4]{0,1:T(4,128)S(1)}, s32[8,4]{0,1:T(4,128)}, u32[]{:S(2)}) copy-start(s32[8,4]{0,1:T(4,128)} %param.3) | copy-start | bytes 388
  72.9 21.0 %collective-permute-start = (bf16[16,10,16,256]{3,2,1,0:T(8,128)(2,1)S(1)}, bf16[16,10,16,256]{3,2,1,0:T(8,128)(2,1)S(1)}, u32[]{:S(2)}, u32[]{:S(2)}) collective-permute-start(bf16[16,10,16,256]{3,2,1,0:T(8,128)(2,1)S(1)} %get-tuple-element.13.sent_across), channel_id=1, source_target_pairs={{1,2},{2,1},{3,4},{4,3},{5,6},{6,5},{7,8},{8,7},{9,10},{10,9},{11,... | collective-permute-start | bytes 3932168 | tf_op jit(solution)/shard_map/ppermute | solution.py:251
  74.8 19.1 %collective-permute-start.1 = (bf16[16,10,16,256]{3,2,1,0:T(8,128)(2,1)S(1)}, bf16[16,10,16,256]{3,2,1,0:T(8,128)(2,1)S(1)}, u32[]{:S(2)}, u32[]{:S(2)}) collective-permute-start(bf16[16,10,16,256]{3,2,1,0:T(8,128)(2,1)S(1)} %get-tuple-element.14.sent_beside), channel_id=1, source_target_pairs={{0,1},{1,0},{2,3},{3,2},{4,5},{5,4},{6,7},{7,6},{8,9},{9,8},{10,11... | collective-permute-start | bytes 3932168 | tf_op jit(solution)/shard_map/ppermute | solution.py:252

commit v5 on v4

--- a/solution.py
+++ b/solution.py
@@ -1,3 +1,5 @@
+import functools
+
 import jax
 import jax.numpy as jnp
 from jax import lax
@@ -5,6 +7,7 @@
 from jax.experimental.pallas import tpu as pltpu
 from jax.sharding import PartitionSpec as P
 
+
 AXES = ("row", "col")
 BLOCK = 256
 BAND = 4
@@ -41,6 +44,10 @@
     return (0.5 * both).astype(jnp.bfloat16)
 
 
+def offchip(array):
+    return pltpu.with_memory_space_constraint(array, pltpu.HBM)
+
+
 def limit(mebibytes):
     return pltpu.CompilerParams(vmem_limit_bytes=mebibytes << 20)
 
@@ -49,55 +56,54 @@
     return pltpu.with_memory_space_constraint(array, pltpu.VMEM)
 
 
-def is_odd():
-    return lax.rem(lax.axis_index("col"), 2)
-
-
-def halo_kernel(occupied, tiles, across, beside, sem):
+def next_side(across):
+    odd = lax.rem(lax.axis_index("col"), 2)
+    return odd if across else 1 - odd
+
+
+def halo_kernel(across, occupied, tiles, out, sem):
     rows = tiles.shape[1]
-    odd = is_odd()
+    upward = next_side(across)
     copies = []
     spans = []
     start = 0
     for m in range(1, BAND + 1):
         count = BAND + 1 - m
-        for target, upward in ((across, odd), (beside, 1 - odd)):
-            row = upward * (rows - m) + (1 - upward) * (m - 1)
-            first = upward * m
-            copies.append(
-                pltpu.make_async_copy(
-                    tiles.at[:, row, pl.ds(first, count)],
-                    target.at[:, pl.ds(start, count)],
-                    sem.at[len(copies)],
-                )
+        row = upward * (rows - m) + (1 - upward) * (m - 1)
+        first = upward * m
+        copies.append(
+            pltpu.make_async_copy(
+                tiles.at[:, row, pl.ds(first, count)],
+                out.at[:, pl.ds(start, count)],
+                sem.at[m - 1],
             )
-            spans.append((target, start, count, row, first))
+        )
+        spans.append((start, count, row, first))
         start += count
     for copy in copies:
         copy.start()
     for copy in copies:
         copy.wait()
-    for target, start, count, row, first in spans:
+    for start, count, row, first in spans:
         for step in range(count):
             d = first + step
             dropped = (d > 0) & jnp.logical_not(keep(occupied, row, jnp.maximum(d, 1)))
 
             @pl.when(dropped)
             def _():
-                target[:, start + step] = jnp.zeros_like(target[:, start + step])
-
-
-def halo_tiles(occupied, tiles):
+                out[:, start + step] = jnp.zeros_like(out[:, start + step])
+
+
+def halo_tiles(across, occupied, tiles):
     parts, _, _, height, width = tiles.shape
-    shape = pltpu.VMEM((parts, len(BELOW), height, width), tiles.dtype)
     return pl.pallas_call(
-        halo_kernel,
-        out_shape=(shape, shape),
+        functools.partial(halo_kernel, across),
+        out_shape=pltpu.VMEM((parts, len(BELOW), height, width), tiles.dtype),
         in_specs=[SCALARS, OFFCHIP],
-        out_specs=(ONCHIP, ONCHIP),
-        scratch_shapes=[pltpu.SemaphoreType.DMA((2 * BAND,))],
+        out_specs=ONCHIP,
+        scratch_shapes=[pltpu.SemaphoreType.DMA((BAND,))],
         compiler_params=limit(4),
-    )(occupied, pltpu.with_memory_space_constraint(tiles, pltpu.HBM))
+    )(occupied, offchip(tiles))
 
 
 def local_kernel(occupied, tiles, out, partial, strips, sem):
@@ -173,67 +179,68 @@
             pltpu.SemaphoreType.DMA((rows, width)),
         ],
         compiler_params=limit(30),
-    )(occupied, pltpu.with_memory_space_constraint(tiles, pltpu.HBM))
-
-
-def border_kernel(occupied, sent_across, sent_beside, across, beside, partial, _, out):
-    odd = is_odd() == 1
-    to_next = (sent_across, sent_beside)
-    below = (beside, across)
-    above = (across, beside)
+    )(occupied, offchip(tiles))
+
+
+def border_kernel(across, occupied, sent, received, partial, _, out):
     parts, rows, _, height, _ = out.shape
     waiting = partial_tiles(rows)
-
-    def get(refs, slot):
-        return jnp.where(odd, refs[0][:, slot], refs[1][:, slot]).reshape(BLOCK, BLOCK)
+    upward = next_side(across)
+
+    def get(ref, slot):
+        return ref[:, slot].reshape(BLOCK, BLOCK)
 
     def finish(i, e, summed):
-        slot = waiting.index((i, e))
-        summed = partial[slot] + summed
+        summed = partial[waiting.index((i, e))] + summed
         if e > 0:
             summed = jnp.where(keep(occupied, i, e), summed, 0.0)
         out[:, i, e] = summed.astype(jnp.bfloat16).reshape(parts, height, BLOCK)
 
-    lower = {
-        j: jnp.concatenate(
-            [get(below, BELOW.index((m, j + m))).T for m in range(BAND - j, 0, -1)], axis=1
-        )
-        for j in range(BAND)
-    }
-    for j in range(BAND):
-        depth = (BAND - j) * BLOCK
-        for i in range(j + 1):
-            rows_i = lower[i][:, lower[i].shape[1] - depth :]
-            finish(i, j - i, times_transposed(rows_i, lower[j]))
-
-    def corner(a, b):
-        if a == b:
-            return symmetric(get(above, ABOVE.index((a, 0))))
-        if a < b:
-            return get(above, ABOVE.index((a, b - a)))
-        return get(above, ABOVE.index((b, a - b))).T
-
-    square = [
-        jnp.concatenate([corner(a, b) for b in range(BAND)], axis=1) for a in range(BAND)
-    ]
-    for i in range(rows - BAND, rows):
-        reach = i + BAND + 1 - rows
-        rows_i = jnp.concatenate(
-            [get(to_next, BELOW.index((rows - i, rows + b - i))) for b in range(reach)], axis=1
-        )
-        for a in range(reach):
-            finish(i, rows + a - i, times_transposed(rows_i, square[a][:, : reach * BLOCK]))
-
-
-def square_border(occupied, halo, partial, product):
+    @pl.when(upward == 0)
+    def _():
+        lower = {
+            j: jnp.concatenate(
+                [get(received, BELOW.index((m, j + m))).T for m in range(BAND - j, 0, -1)],
+                axis=1,
+            )
+            for j in range(BAND)
+        }
+        for j in range(BAND):
+            depth = (BAND - j) * BLOCK
+            for i in range(j + 1):
+                rows_i = lower[i][:, lower[i].shape[1] - depth :]
+                finish(i, j - i, times_transposed(rows_i, lower[j]))
+
+    @pl.when(upward == 1)
+    def _():
+        def corner(a, b):
+            if a == b:
+                return symmetric(get(received, ABOVE.index((a, 0))))
+            if a < b:
+                return get(received, ABOVE.index((a, b - a)))
+            return get(received, ABOVE.index((b, a - b))).T
+
+        square = [
+            jnp.concatenate([corner(a, b) for b in range(BAND)], axis=1) for a in range(BAND)
+        ]
+        for i in range(rows - BAND, rows):
+            reach = i + BAND + 1 - rows
+            rows_i = jnp.concatenate(
+                [get(sent, BELOW.index((rows - i, rows + b - i))) for b in range(reach)], axis=1
+            )
+            for a in range(reach):
+                finish(i, rows + a - i, times_transposed(rows_i, square[a][:, : reach * BLOCK]))
+
+
+def square_border(across, occupied, sent, received, partial, product):
     return pl.pallas_call(
-        border_kernel,
+        functools.partial(border_kernel, across),
         out_shape=pltpu.VMEM(product.shape, product.dtype),
-        in_specs=[SCALARS] + [ONCHIP] * 6,
+        in_specs=[SCALARS] + [ONCHIP] * 4,
         out_specs=ONCHIP,
-        input_output_aliases={6: 0},
+        input_output_aliases={4: 0},
         compiler_params=limit(20),
-    )(occupied, *(onchip(a) for a in (*halo, partial, product)))
+    )(occupied, *(onchip(a) for a in (sent, received, partial, product)))
 
 
 def swaps(firsts):
@@ -247,12 +254,13 @@
     tiles = upper_tiles.reshape((parts, rows) + upper_tiles.shape[1:])
     tiles = lax.all_to_all(tiles, "col", 0, 0, tiled=True)
     tiles, occupied = lax.optimization_barrier((tiles, occupied))
-    sent_across, sent_beside = halo_tiles(occupied, tiles)
+    sent_across = halo_tiles(True, occupied, tiles)
     across = lax.ppermute(sent_across, AXES, swaps(range(1, count - 1, 2)))
+    sent_beside = halo_tiles(False, occupied, tiles)
     beside = lax.ppermute(sent_beside, AXES, swaps(range(0, count, 2)))
     product, partial = square_local(occupied, tiles)
-    halo = (sent_across, sent_beside, across, beside)
-    product = square_border(occupied, halo, partial, product)
+    product = square_border(False, occupied, sent_beside, beside, partial, product)
+    product = square_border(True, occupied, sent_across, across, partial, product)
     product = lax.all_to_all(product, "col", 0, 0, tiled=True)
     return product.reshape(upper_tiles.shape)
 

time: 168 us -> 168 us (level)
  Pallas kernels: 17.9 us -> 20 us
  waiting for transfers between devices: 6.66 us -> 4.82 us
    pallas_call x2 -> x4, Pallas kernels: 5.52 us -> 7.67 us  [the longest x2 4.18 us: halo_tiles(): pl.pallas_call(functools.partial(halo_kernel, across), out_shape=pltpu.VM...]
    ppermute x1, waiting for transfers between devices: 6.66 us -> 4.82 us  [shards(): across = lax.ppermute(sent_across, AXES, swaps(range(1, count - 1, 2)))]
  transfers between devices with their start and end apart: 2 -> 2, of which waited for: 1 -> 1; matrix products, arithmetic and copies ran while one was open for 0% -> 0% of each run, Pallas kernels for 7% -> 10%
where the time goes in v5:
time: 168 us; the launch traced here: 167 us
  blocking collectives  138 us (82%)
  Pallas kernels  20 us (12%)
  waiting for transfers between devices  4.82 us (3%)
  local copies, waits for them, and re-layouts  2.44 us (1%)
  starting transfers between devices  2.01 us (1%)
    all_to_all x1, blocking collectives, shards(): tiles = lax.all_to_all(tiles, 'col', 0, 0, tiled=True)  70.1 us
    all_to_all x1, blocking collectives, shards(): product = lax.all_to_all(product, 'col', 0, 0, tiled=True)  67.4 us
    pallas_call x1, Pallas kernels, square_local(): pl.pallas_call(local_kernel, out_shape=(pltpu.VMEM(tiles.shape, jnp.bfloa...  12.4 us
    ppermute x1, waiting for transfers between devices, shards(): across = lax.ppermute(sent_across, AXES, swaps(range(1, count - 1, 2)))  4.82 us
    pallas_call x2, Pallas kernels, halo_tiles(): pl.pallas_call(functools.partial(halo_kernel, across), out_shape=pltpu.VM...  4.18 us
    pallas_call x2, Pallas kernels, square_border(): pl.pallas_call(functools.partial(border_kernel, across), out_shape=pltpu....  3.49 us
  transfers between devices with their start and end apart: 2, of which 1 were waited for; matrix products, arithmetic and copies ran while one was open for 0% of the time, Pallas kernels for 10%

profile of v5, /device:TPU:34, one launch (start us, length us, event | category | flops | bytes accessed | tf_op | source)
XLA Modules:
  0.0 166.9 jit_solution(17477469898558492335)
XLA Ops:
  0.0 0.0 copy-start
  0.0 70.1 %all_to_all.10.tiles = bf16[16,8,5,16,256]{4,3,2,1,0:T(8,128)(2,1)} all-to-all(bf16[16,8,5,16,256]{4,3,2,1,0:T(8,128)(2,1)} %bitcast.3), channel_id=1, replica_groups=mesh['row'=8,'col'=16] {'col'}, dimensions={0} | all-to-all | bytes 10485760 | tf_op jit(solution)/shard_map/all_to_all | solution.py:255
  70.1 0.0 copy-done
  70.1 0.1 copy.9.occupied
  70.2 2.1 %shard_map.30.sent = bf16[16,10,16,256]{3,2,1,0:T(8,128)(2,1)S(1)} custom-call(s32[8,4]{1,0:T(8,128)S(1)} %copy.9.occupied, bf16[16,8,5,16,256]{4,3,2,1,0:T(8,128)(2,1)} %all_to_all.10.tiles), custom_call_target="tpu_custom_call" | custom-call | tf_op jit(solution)/shard_map/pallas_call | solution.py:99
  72.3 0.1 collective-permute-start.1
  72.4 2.1 %shard_map.28.sent = bf16[16,10,16,256]{3,2,1,0:T(8,128)(2,1)S(1)} custom-call(s32[8,4]{1,0:T(8,128)S(1)} %copy.9.occupied, bf16[16,8,5,16,256]{4,3,2,1,0:T(8,128)(2,1)} %all_to_all.10.tiles), custom_call_target="tpu_custom_call" | custom-call | tf_op jit(solution)/shard_map/pallas_call | solution.py:99
  74.5 1.9 %collective-permute-start = (bf16[16,10,16,256]{3,2,1,0:T(8,128)(2,1)S(1)}, bf16[16,10,16,256]{3,2,1,0:T(8,128)(2,1)S(1)}, u32[]{:S(2)}, u32[]{:S(2)}) collective-permute-start(bf16[16,10,16,256]{3,2,1,0:T(8,128)(2,1)S(1)} %shard_map.28.sent), channel_id=1, source_target_pairs={{1,2},{2,1},{3,4},{4,3},{5,6},{6,5},{7,8},{8,7},{9,10},{10,9},{11,... | collective-permute-start | bytes 3932168 | tf_op jit(solution)/shard_map/ppermute | solution.py:258
  76.4 12.4 %shard_map.29 = (bf16[16,8,5,16,256]{4,3,2,1,0:T(8,128)(2,1)S(1)}, f32[20,256,256]{2,1,0:T(8,128)S(1)}) custom-call(s32[8,4]{1,0:T(8,128)S(1)} %copy.9.occupied, bf16[16,8,5,16,256]{4,3,2,1,0:T(8,128)(2,1)} %all_to_all.10.tiles), custom_call_target="tpu_custom_call" | custom-call | tf_op jit(solution)/shard_map/pallas_call | solution.py:169
  88.8 0.0 collective-permute-done.1.received
  88.8 1.9 %shard_map.31._ = bf16[16,8,5,16,256]{4,3,2,1,0:T(8,128)(2,1)S(1)} custom-call(s32[8,4]{1,0:T(8,128)S(1)} %copy.9.occupied, bf16[16,10,16,256]{3,2,1,0:T(8,128)(2,1)S(1)} %shard_map.30.sent, bf16[16,10,16,256]{3,2,1,0:T(8,128)(2,1)S(1)} %collective-permute-done.1.received, ...), custom_call_target="tpu_custom_call", output_to_operand_aliasing={{}: (4, {})} | custom-call | tf_op jit(solution)/shard_map/pallas_call | solution.py:236
  90.7 4.8 %collective-permute-done.received = bf16[16,10,16,256]{3,2,1,0:T(8,128)(2,1)S(1)} collective-permute-done((bf16[16,10,16,256]{3,2,1,0:T(8,128)(2,1)S(1)}, bf16[16,10,16,256]{3,2,1,0:T(8,128)(2,1)S(1)}, u32[]{:S(2)}, u32[]{:S(2)}) %collective-permute-start) | collective-permute-done | bytes 1310752 | tf_op jit(solution)/shard_map/ppermute | solution.py:258
  95.5 1.6 shard_map.32
  97.1 67.4 %all_to_all.11 = bf16[16,8,5,16,256]{4,3,2,1,0:T(8,128)(2,1)S(1)} all-to-all(bf16[16,8,5,16,256]{4,3,2,1,0:T(8,128)(2,1)S(1)} %shard_map.32), channel_id=1, replica_groups=mesh['row'=8,'col'=16] {'col'}, dimensions={0} | all-to-all | bytes 10485760 | tf_op jit(solution)/shard_map/all_to_all | solution.py:264
  164.5 2.4 %copy.13 = bf16[128,5,16,256]{3,2,1,0:T(8,128)(2,1)} copy(bf16[128,5,16,256]{3,2,1,0:T(8,128)(2,1)S(1)} %bitcast.2) | data formatting | bytes 10485760
Async XLA Ops:
  0.0 70.1 %copy-start = (s32[8,4]{0,1:T(4,128)S(1)}, s32[8,4]{0,1:T(4,128)}, u32[]{:S(2)}) copy-start(s32[8,4]{0,1:T(4,128)} %param.3) | copy-start | bytes 388
  72.3 16.5 %collective-permute-start.1 = (bf16[16,10,16,256]{3,2,1,0:T(8,128)(2,1)S(1)}, bf16[16,10,16,256]{3,2,1,0:T(8,128)(2,1)S(1)}, u32[]{:S(2)}, u32[]{:S(2)}) collective-permute-start(bf16[16,10,16,256]{3,2,1,0:T(8,128)(2,1)S(1)} %shard_map.30.sent), channel_id=1, source_target_pairs={{0,1},{1,0},{2,3},{3,2},{4,5},{5,4},{6,7},{7,6},{8,9},{9,8},{10,11... | collective-permute-start | bytes 3932168 | tf_op jit(solution)/shard_map/ppermute | solution.py:260
  74.5 21.0 %collective-permute-start = (bf16[16,10,16,256]{3,2,1,0:T(8,128)(2,1)S(1)}, bf16[16,10,16,256]{3,2,1,0:T(8,128)(2,1)S(1)}, u32[]{:S(2)}, u32[]{:S(2)}) collective-permute-start(bf16[16,10,16,256]{3,2,1,0:T(8,128)(2,1)S(1)} %shard_map.28.sent), channel_id=1, source_target_pairs={{1,2},{2,1},{3,4},{4,3},{5,6},{6,5},{7,8},{8,7},{9,10},{10,9},{11,... | collective-permute-start | bytes 3932168 | tf_op jit(solution)/shard_map/ppermute | solution.py:258

commit v6 on v5

--- a/solution.py
+++ b/solution.py
@@ -16,7 +16,6 @@
 ABOVE = [(m, d) for m in range(BAND) for d in range(BAND - m)]
 
 SCALARS = pl.BlockSpec(memory_space=pltpu.SMEM)
-OFFCHIP = pl.BlockSpec(memory_space=pltpu.HBM)
 ONCHIP = pl.BlockSpec(memory_space=pltpu.VMEM)
 
 
@@ -27,10 +26,10 @@
 
 
 def keep(occupied, row, d):
-    rows = occupied.shape[0]
+    rows = occupied.shape[1]
     here = lax.axis_index("row") * lax.axis_size("col") + lax.axis_index("col")
     there = lax.axis_size("row") * lax.axis_size("col")
-    return (occupied[row, d - 1] == 1) & (here * rows + row + d < there * rows)
+    return (occupied[d - 1, row] == 1) & (here * rows + row + d < there * rows)
 
 
 def times_transposed(left, right):
@@ -44,10 +43,6 @@
     return (0.5 * both).astype(jnp.bfloat16)
 
 
-def offchip(array):
-    return pltpu.with_memory_space_constraint(array, pltpu.HBM)
-
-
 def limit(mebibytes):
     return pltpu.CompilerParams(vmem_limit_bytes=mebibytes << 20)
 
@@ -61,87 +56,61 @@
     return odd if across else 1 - odd
 
 
-def halo_kernel(across, occupied, tiles, out, sem):
+def kept_tile(occupied, tiles, row, d):
+    tile = tiles[:, row, d]
+    return jnp.where(keep(occupied, row, d), tile, jnp.zeros_like(tile))
+
+
+def halo_kernel(occupied, tiles, across, beside, _):
     rows = tiles.shape[1]
-    upward = next_side(across)
-    copies = []
-    spans = []
-    start = 0
-    for m in range(1, BAND + 1):
-        count = BAND + 1 - m
-        row = upward * (rows - m) + (1 - upward) * (m - 1)
-        first = upward * m
-        copies.append(
-            pltpu.make_async_copy(
-                tiles.at[:, row, pl.ds(first, count)],
-                out.at[:, pl.ds(start, count)],
-                sem.at[m - 1],
-            )
-        )
-        spans.append((start, count, row, first))
-        start += count
-    for copy in copies:
-        copy.start()
-    for copy in copies:
-        copy.wait()
-    for start, count, row, first in spans:
-        for step in range(count):
-            d = first + step
-            dropped = (d > 0) & jnp.logical_not(keep(occupied, row, jnp.maximum(d, 1)))
-
-            @pl.when(dropped)
-            def _():
-                out[:, start + step] = jnp.zeros_like(out[:, start + step])
-
-
-def halo_tiles(across, occupied, tiles):
+    odd = next_side(True)
+
+    def gather(to_next, to_last):
+        for slot, (m, d) in enumerate(BELOW):
+            to_next[:, slot] = kept_tile(occupied, tiles, rows - m, d)
+        for slot, (m, d) in enumerate(ABOVE):
+            to_last[:, slot] = kept_tile(occupied, tiles, m, d) if d else tiles[:, m, d]
+
+    @pl.when(odd == 1)
+    def _():
+        gather(across, beside)
+
+    @pl.when(odd == 0)
+    def _():
+        gather(beside, across)
+
+
+def halo_tiles(occupied, tiles):
     parts, _, _, height, width = tiles.shape
+    halo = pltpu.VMEM((parts, len(BELOW), height, width), tiles.dtype)
     return pl.pallas_call(
-        functools.partial(halo_kernel, across),
-        out_shape=pltpu.VMEM((parts, len(BELOW), height, width), tiles.dtype),
-        in_specs=[SCALARS, OFFCHIP],
-        out_specs=ONCHIP,
-        scratch_shapes=[pltpu.SemaphoreType.DMA((BAND,))],
-        compiler_params=limit(4),
-    )(occupied, offchip(tiles))
-
-
-def local_kernel(occupied, tiles, out, partial, strips, sem):
+        halo_kernel,
+        out_shape=(halo, halo, pltpu.VMEM(tiles.shape, tiles.dtype)),
+        in_specs=[SCALARS, ONCHIP],
+        out_specs=(ONCHIP,) * 3,
+        input_output_aliases={1: 2},
+        compiler_params=limit(2),
+    )(occupied, onchip(tiles))
+
+
+def local_kernel(occupied, tiles, out, partial, strips):
     parts, rows, _, height, _ = tiles.shape
     waiting = partial_tiles(rows)
 
     def block(row, d):
         return strips.at[row, :, :, pl.ds((BAND + d) * BLOCK, BLOCK)]
 
-    def load(row, d):
-        return pltpu.make_async_copy(tiles.at[:, row, d], block(row, d), sem.at[row, d])
-
-    def get(row, d):
-        return block(row, d)[...].reshape(BLOCK, BLOCK)
-
     def put(row, d, value):
         block(row, d)[...] = value.reshape(parts, height, BLOCK)
 
-    for row in range(rows):
-        for d in range(BAND + 1):
-            load(row, d).start()
-
-    def arrive(row):
-        for d in range(BAND + 1):
-            load(row, d).wait()
-            if d > 0:
-
-                @pl.when(jnp.logical_not(keep(occupied, row, d)))
-                def _():
-                    put(row, d, jnp.zeros((BLOCK, BLOCK), jnp.bfloat16))
-
     def prepare(j):
         if j < rows:
-            arrive(j)
-            put(j, 0, symmetric(get(j, 0)))
+            put(j, 0, symmetric(tiles[:, j, 0].reshape(BLOCK, BLOCK)))
+            for d in range(1, BAND + 1):
+                put(j, d, kept_tile(occupied, tiles, j, d))
         for m in range(1, BAND + 1):
             if 0 <= j - m < rows:
-                put(j, -m, get(j - m, m).T)
+                put(j, -m, block(j - m, m)[...].reshape(BLOCK, BLOCK).T)
 
     for j in range(BAND):
         prepare(j)
@@ -164,7 +133,7 @@
 
 
 def square_local(occupied, tiles):
-    parts, rows, width, height, _ = tiles.shape
+    parts, rows, _, height, _ = tiles.shape
     count = len(partial_tiles(rows))
     return pl.pallas_call(
         local_kernel,
@@ -172,14 +141,13 @@
             pltpu.VMEM(tiles.shape, jnp.bfloat16),
             pltpu.VMEM((count, BLOCK, BLOCK), jnp.float32),
         ),
-        in_specs=[SCALARS, OFFCHIP],
+        in_specs=[SCALARS, ONCHIP],
         out_specs=(ONCHIP, ONCHIP),
         scratch_shapes=[
             pltpu.VMEM((rows + BAND, parts, height, LANES), jnp.bfloat16),
-            pltpu.SemaphoreType.DMA((rows, width)),
         ],
-        compiler_params=limit(30),
-    )(occupied, offchip(tiles))
+        compiler_params=limit(18),
+    )(occupied, onchip(tiles))
 
 
 def border_kernel(across, occupied, sent, received, partial, _, out):
@@ -239,7 +207,7 @@
         in_specs=[SCALARS] + [ONCHIP] * 4,
         out_specs=ONCHIP,
         input_output_aliases={4: 0},
-        compiler_params=limit(20),
+        compiler_params=limit(8),
     )(occupied, *(onchip(a) for a in (sent, received, partial, product)))
 
 
@@ -253,10 +221,9 @@
     rows = occupied.shape[0]
     tiles = upper_tiles.reshape((parts, rows) + upper_tiles.shape[1:])
     tiles = lax.all_to_all(tiles, "col", 0, 0, tiled=True)
-    tiles, occupied = lax.optimization_barrier((tiles, occupied))
-    sent_across = halo_tiles(True, occupied, tiles)
+    occupied = occupied.T
+    sent_across, sent_beside, tiles = halo_tiles(occupied, tiles)
     across = lax.ppermute(sent_across, AXES, swaps(range(1, count - 1, 2)))
-    sent_beside = halo_tiles(False, occupied, tiles)
     beside = lax.ppermute(sent_beside, AXES, swaps(range(0, count, 2)))
     product, partial = square_local(occupied, tiles)
     product = square_border(False, occupied, sent_beside, beside, partial, product)

time: 168 us -> 165 us (0.982)
  Pallas kernels: 20 us -> 13 us
  waiting for transfers between devices: 4.82 us -> 8.47 us
    ppermute x1, waiting for transfers between devices: 4.82 us -> 8.47 us  [shards(): across = lax.ppermute(sent_across, AXES, swaps(range(1, count - 1, 2)))]
    pallas_call x1, Pallas kernels: 12.4 us -> 8.74 us  [square_local(): pl.pallas_call(local_kernel, out_shape=(pltpu.VMEM(tiles.shape, jnp.bfloa...]
    pallas_call x2 -> x1, Pallas kernels: 4.18 us -> 0.87 us  [halo_tiles(): pl.pallas_call(halo_kernel, out_shape=(halo, halo, pltpu.VMEM(tiles.shape...]
  transfers between devices with their start and end apart: 2 -> 2, of which waited for: 1 -> 1; matrix products, arithmetic and copies ran while one was open for 0% -> 0% of each run, Pallas kernels for 10% -> 6%
where the time goes in v6:
time: 165 us; the launch traced here: 163 us
  blocking collectives  137 us (83%)
  Pallas kernels  13 us (8%)
  waiting for transfers between devices  8.47 us (5%)
  local copies, waits for them, and re-layouts  2.36 us (1%)
  starting transfers between devices  2.01 us (1%)
    all_to_all x1, blocking collectives, shards(): tiles = lax.all_to_all(tiles, 'col', 0, 0, tiled=True)  70 us
    all_to_all x1, blocking collectives, shards(): product = lax.all_to_all(product, 'col', 0, 0, tiled=True)  67.5 us
    pallas_call x1, Pallas kernels, square_local(): pl.pallas_call(local_kernel, out_shape=(pltpu.VMEM(tiles.shape, jnp.bfloa...  8.74 us
    ppermute x1, waiting for transfers between devices, shards(): across = lax.ppermute(sent_across, AXES, swaps(range(1, count - 1, 2)))  8.47 us
    pallas_call x2, Pallas kernels, square_border(): pl.pallas_call(functools.partial(border_kernel, across), out_shape=pltpu....  3.42 us
  transfers between devices with their start and end apart: 2, of which 1 were waited for; matrix products, arithmetic and copies ran while one was open for 0% of the time, Pallas kernels for 6%

profile of v6, /device:TPU:34, one launch (start us, length us, event | category | flops | bytes accessed | tf_op | source)
XLA Modules:
  0.0 163.4 jit_solution(7375190840487151609)
XLA Ops:
  0.0 0.0 copy-start
  0.0 70.0 %all_to_all.10.tiles = bf16[16,8,5,16,256]{4,3,2,1,0:T(8,128)(2,1)S(1)} all-to-all(bf16[16,8,5,16,256]{4,3,2,1,0:T(8,128)(2,1)} %bitcast.8), channel_id=1, replica_groups=mesh['row'=8,'col'=16] {'col'}, dimensions={0} | all-to-all | bytes 10485760 | tf_op jit(solution)/shard_map/all_to_all | solution.py:223
  70.0 0.0 copy-done
  70.0 0.9 shard_map.28
  70.9 0.1 collective-permute-start.1
  71.0 1.9 %collective-permute-start = (bf16[16,10,16,256]{3,2,1,0:T(8,128)(2,1)S(1)}, bf16[16,10,16,256]{3,2,1,0:T(8,128)(2,1)S(1)}, u32[]{:S(2)}, u32[]{:S(2)}) collective-permute-start(bf16[16,10,16,256]{3,2,1,0:T(8,128)(2,1)S(1)} %get-tuple-element.10.sent), channel_id=1, source_target_pairs={{1,2},{2,1},{3,4},{4,3},{5,6},{6,5},{7,8},{8,7},{9,10},{10,9},{11,... | collective-permute-start | bytes 3932168 | tf_op jit(solution)/shard_map/ppermute | solution.py:226
  72.9 8.7 %shard_map.29 = (bf16[16,8,5,16,256]{4,3,2,1,0:T(8,128)(2,1)S(1)}, f32[20,256,256]{2,1,0:T(8,128)S(1)}) custom-call(s32[4,8]{1,0:T(4,128)S(1)} %bitcast.4, bf16[16,8,5,16,256]{4,3,2,1,0:T(8,128)(2,1)S(1)} %get-tuple-element.11.tiles), custom_call_target="tpu_custom_call" | custom-call | tf_op jit(solution)/shard_map/pallas_call | solution.py:138
  81.7 0.0 collective-permute-done.1.received
  81.7 1.9 %shard_map.30._ = bf16[16,8,5,16,256]{4,3,2,1,0:T(8,128)(2,1)S(1)} custom-call(s32[4,8]{1,0:T(4,128)S(1)} %bitcast.5, bf16[16,10,16,256]{3,2,1,0:T(8,128)(2,1)S(1)} %get-tuple-element.13.sent, bf16[16,10,16,256]{3,2,1,0:T(8,128)(2,1)S(1)} %collective-permute-done.1.received, ...), custom_call_target="tpu_custom_call", output_to_operand_aliasing={{}: (4, {})} | custom-call | tf_op jit(solution)/shard_map/pallas_call | solution.py:204
  83.6 8.5 %collective-permute-done.received = bf16[16,10,16,256]{3,2,1,0:T(8,128)(2,1)S(1)} collective-permute-done((bf16[16,10,16,256]{3,2,1,0:T(8,128)(2,1)S(1)}, bf16[16,10,16,256]{3,2,1,0:T(8,128)(2,1)S(1)}, u32[]{:S(2)}, u32[]{:S(2)}) %collective-permute-start) | collective-permute-done | bytes 1310752 | tf_op jit(solution)/shard_map/ppermute | solution.py:226
  92.0 1.5 shard_map.31
  93.6 67.5 %all_to_all.11 = bf16[16,8,5,16,256]{4,3,2,1,0:T(8,128)(2,1)S(1)} all-to-all(bf16[16,8,5,16,256]{4,3,2,1,0:T(8,128)(2,1)S(1)} %shard_map.31), channel_id=1, replica_groups=mesh['row'=8,'col'=16] {'col'}, dimensions={0} | all-to-all | bytes 10485760 | tf_op jit(solution)/shard_map/all_to_all | solution.py:231
  161.0 2.4 %copy.10 = bf16[128,5,16,256]{3,2,1,0:T(8,128)(2,1)} copy(bf16[128,5,16,256]{3,2,1,0:T(8,128)(2,1)S(1)} %bitcast.7) | data formatting | bytes 10485760
Async XLA Ops:
  0.0 70.0 %copy-start = (s32[8,4]{0,1:T(4,128)S(1)}, s32[8,4]{0,1:T(4,128)}, u32[]{:S(2)}) copy-start(s32[8,4]{0,1:T(4,128)} %param.3) | copy-start | bytes 388
  70.9 10.8 %collective-permute-start.1 = (bf16[16,10,16,256]{3,2,1,0:T(8,128)(2,1)S(1)}, bf16[16,10,16,256]{3,2,1,0:T(8,128)(2,1)S(1)}, u32[]{:S(2)}, u32[]{:S(2)}) collective-permute-start(bf16[16,10,16,256]{3,2,1,0:T(8,128)(2,1)S(1)} %get-tuple-element.13.sent), channel_id=1, source_target_pairs={{0,1},{1,0},{2,3},{3,2},{4,5},{5,4},{6,7},{7,6},{8,9},{9,8},{10,11... | collective-permute-start | bytes 3932168 | tf_op jit(solution)/shard_map/ppermute | solution.py:227
  71.0 21.0 %collective-permute-start = (bf16[16,10,16,256]{3,2,1,0:T(8,128)(2,1)S(1)}, bf16[16,10,16,256]{3,2,1,0:T(8,128)(2,1)S(1)}, u32[]{:S(2)}, u32[]{:S(2)}) collective-permute-start(bf16[16,10,16,256]{3,2,1,0:T(8,128)(2,1)S(1)} %get-tuple-element.10.sent), channel_id=1, source_target_pairs={{1,2},{2,1},{3,4},{4,3},{5,6},{6,5},{7,8},{8,7},{9,10},{10,9},{11,... | collective-permute-start | bytes 3932168 | tf_op jit(solution)/shard_map/ppermute | solution.py:226

commit v7 on v6

--- a/solution.py
+++ b/solution.py
@@ -25,11 +25,34 @@
     ]
 
 
-def keep(occupied, row, d):
+def chain(parts):
+    half = parts // 2
+    return list(range(half)) + [half + parts - 2 - c + 2 * (c % 2) for c in range(half, parts)]
+
+
+def place(array):
+    pieces = []
+    for part in chain(array.shape[0]):
+        if pieces and part == pieces[-1][1]:
+            pieces[-1][1] = part + 1
+        else:
+            pieces.append([part, part + 1])
+    return jnp.concatenate([array[first:last] for first, last in pieces], axis=0)
+
+
+def seat():
+    parts = lax.axis_size("col")
+    half = parts // 2
+    col = lax.axis_index("col")
+    late = col // half
+    mirrored = half + parts - 2 - col + 2 * lax.rem(col, 2)
+    return lax.axis_index("row") * parts + (1 - late) * col + late * mirrored
+
+
+def keep(occupied, row, d, away=0):
     rows = occupied.shape[1]
-    here = lax.axis_index("row") * lax.axis_size("col") + lax.axis_index("col")
-    there = lax.axis_size("row") * lax.axis_size("col")
-    return (occupied[d - 1, row] == 1) & (here * rows + row + d < there * rows)
+    total = lax.axis_size("row") * lax.axis_size("col") * rows
+    return (occupied[d - 1, row] == 1) & ((seat() + away) * rows + row + d < total)
 
 
 def times_transposed(left, right):
@@ -56,20 +79,19 @@
     return odd if across else 1 - odd
 
 
-def kept_tile(occupied, tiles, row, d):
-    tile = tiles[:, row, d]
-    return jnp.where(keep(occupied, row, d), tile, jnp.zeros_like(tile))
-
-
-def halo_kernel(occupied, tiles, across, beside, _):
+def kept_tile(occupied, tile, row, d, away=0):
+    return jnp.where(keep(occupied, row, d, away), tile, jnp.zeros_like(tile))
+
+
+def halo_kernel(tiles, across, beside, _):
     rows = tiles.shape[1]
     odd = next_side(True)
 
     def gather(to_next, to_last):
         for slot, (m, d) in enumerate(BELOW):
-            to_next[:, slot] = kept_tile(occupied, tiles, rows - m, d)
+            to_next[:, slot] = place(tiles[:, rows - m, d])
         for slot, (m, d) in enumerate(ABOVE):
-            to_last[:, slot] = kept_tile(occupied, tiles, m, d) if d else tiles[:, m, d]
+            to_last[:, slot] = place(tiles[:, m, d])
 
     @pl.when(odd == 1)
     def _():
@@ -80,17 +102,17 @@
         gather(beside, across)
 
 
-def halo_tiles(occupied, tiles):
+def halo_tiles(tiles):
     parts, _, _, height, width = tiles.shape
     halo = pltpu.VMEM((parts, len(BELOW), height, width), tiles.dtype)
     return pl.pallas_call(
         halo_kernel,
         out_shape=(halo, halo, pltpu.VMEM(tiles.shape, tiles.dtype)),
-        in_specs=[SCALARS, ONCHIP],
+        in_specs=[ONCHIP],
         out_specs=(ONCHIP,) * 3,
-        input_output_aliases={1: 2},
+        input_output_aliases={0: 2},
         compiler_params=limit(2),
-    )(occupied, onchip(tiles))
+    )(onchip(tiles))
 
 
 def local_kernel(occupied, tiles, out, partial, strips):
@@ -105,9 +127,9 @@
 
     def prepare(j):
         if j < rows:
-            put(j, 0, symmetric(tiles[:, j, 0].reshape(BLOCK, BLOCK)))
+            put(j, 0, symmetric(place(tiles[:, j, 0]).reshape(BLOCK, BLOCK)))
             for d in range(1, BAND + 1):
-                put(j, d, kept_tile(occupied, tiles, j, d))
+                put(j, d, kept_tile(occupied, place(tiles[:, j, d]), j, d))
         for m in range(1, BAND + 1):
             if 0 <= j - m < rows:
                 put(j, -m, block(j - m, m)[...].reshape(BLOCK, BLOCK).T)
@@ -129,7 +151,7 @@
             else:
                 if e > 0:
                     summed = jnp.where(keep(occupied, i, e), summed, 0.0)
-                out[:, i, e] = summed.astype(jnp.bfloat16).reshape(parts, height, BLOCK)
+                out[:, i, e] = place(summed.astype(jnp.bfloat16).reshape(parts, height, BLOCK))
 
 
 def square_local(occupied, tiles):
@@ -150,25 +172,36 @@
     )(occupied, onchip(tiles))
 
 
-def border_kernel(across, occupied, sent, received, partial, _, out):
+def border_kernel(across, occupied, theirs, sent, received, partial, _, out):
     parts, rows, _, height, _ = out.shape
     waiting = partial_tiles(rows)
     upward = next_side(across)
 
-    def get(ref, slot):
-        return ref[:, slot].reshape(BLOCK, BLOCK)
+    def below(m, d):
+        tile = kept_tile(theirs, received[:, BELOW.index((m, d))], rows - m, d, -1)
+        return tile.reshape(BLOCK, BLOCK)
+
+    def above(m, d):
+        tile = received[:, ABOVE.index((m, d))]
+        if d:
+            tile = kept_tile(theirs, tile, m, d, 1)
+        return tile.reshape(BLOCK, BLOCK)
+
+    def own(m, d):
+        tile = kept_tile(occupied, sent[:, BELOW.index((m, d))], rows - m, d)
+        return tile.reshape(BLOCK, BLOCK)
 
     def finish(i, e, summed):
         summed = partial[waiting.index((i, e))] + summed
         if e > 0:
             summed = jnp.where(keep(occupied, i, e), summed, 0.0)
-        out[:, i, e] = summed.astype(jnp.bfloat16).reshape(parts, height, BLOCK)
+        out[:, i, e] = place(summed.astype(jnp.bfloat16).reshape(parts, height, BLOCK))
 
     @pl.when(upward == 0)
     def _():
         lower = {
             j: jnp.concatenate(
-                [get(received, BELOW.index((m, j + m))).T for m in range(BAND - j, 0, -1)],
+                [below(m, j + m).T for m in range(BAND - j, 0, -1)],
                 axis=1,
             )
             for j in range(BAND)
@@ -183,10 +216,10 @@
     def _():
         def corner(a, b):
             if a == b:
-                return symmetric(get(received, ABOVE.index((a, 0))))
+                return symmetric(above(a, 0))
             if a < b:
-                return get(received, ABOVE.index((a, b - a)))
-            return get(received, ABOVE.index((b, a - b))).T
+                return above(a, b - a)
+            return above(b, a - b).T
 
         square = [
             jnp.concatenate([corner(a, b) for b in range(BAND)], axis=1) for a in range(BAND)
@@ -194,42 +227,51 @@
         for i in range(rows - BAND, rows):
             reach = i + BAND + 1 - rows
             rows_i = jnp.concatenate(
-                [get(sent, BELOW.index((rows - i, rows + b - i))) for b in range(reach)], axis=1
+                [own(rows - i, rows + b - i) for b in range(reach)], axis=1
             )
             for a in range(reach):
                 finish(i, rows + a - i, times_transposed(rows_i, square[a][:, : reach * BLOCK]))
 
 
-def square_border(across, occupied, sent, received, partial, product):
+def square_border(across, occupied, theirs, sent, received, partial, product):
     return pl.pallas_call(
         functools.partial(border_kernel, across),
         out_shape=pltpu.VMEM(product.shape, product.dtype),
-        in_specs=[SCALARS] + [ONCHIP] * 4,
+        in_specs=[SCALARS] * 2 + [ONCHIP] * 4,
         out_specs=ONCHIP,
-        input_output_aliases={4: 0},
+        input_output_aliases={5: 0},
         compiler_params=limit(8),
-    )(occupied, *(onchip(a) for a in (sent, received, partial, product)))
-
-
-def swaps(firsts):
-    return [pair for p in firsts for pair in ((p, p + 1), (p + 1, p))]
+    )(occupied, theirs, *(onchip(a) for a in (sent, received, partial, product)))
+
+
+def exchange(array):
+    parts = lax.axis_size("col")
+    return lax.all_to_all(array, "col", 0, 0, axis_index_groups=[chain(parts)], tiled=True)
 
 
 def shards(upper_tiles, occupied):
     parts = lax.axis_size("col")
     count = lax.axis_size("row") * parts
     rows = occupied.shape[0]
-    tiles = upper_tiles.reshape((parts, rows) + upper_tiles.shape[1:])
-    tiles = lax.all_to_all(tiles, "col", 0, 0, tiled=True)
+    device = [p // parts * parts + chain(parts)[p % parts] for p in range(count)]
+    facing = [(p, p + 1 if p % 2 else p - 1) for p in range(1, count - 1)]
+    paired = [(p, p ^ 1) for p in range(count)]
+
+    def swap(array, places):
+        return lax.ppermute(array, AXES, [(device[p], device[q]) for p, q in places])
+
+    tiles = exchange(upper_tiles.reshape((parts, rows) + upper_tiles.shape[1:]))
+    sent_across, sent_beside, tiles = halo_tiles(tiles)
+    across = swap(sent_across, facing)
+    beside = swap(sent_beside, paired)
     occupied = occupied.T
-    sent_across, sent_beside, tiles = halo_tiles(occupied, tiles)
-    across = lax.ppermute(sent_across, AXES, swaps(range(1, count - 1, 2)))
-    beside = lax.ppermute(sent_beside, AXES, swaps(range(0, count, 2)))
-    product, partial = square_local(occupied, tiles)
-    product = square_border(False, occupied, sent_beside, beside, partial, product)
-    product = square_border(True, occupied, sent_across, across, partial, product)
-    product = lax.all_to_all(product, "col", 0, 0, tiled=True)
-    return product.reshape(upper_tiles.shape)
+    own = lax.ppermute(occupied, AXES, [(p, device[p]) for p in range(count)])
+    near = lax.ppermute(occupied, AXES, [(p, device[q]) for p, q in paired])
+    far = lax.ppermute(occupied, AXES, [(p, device[q]) for p, q in facing])
+    product, partial = square_local(own, tiles)
+    product = square_border(False, own, near, sent_beside, beside, partial, product)
+    product = square_border(True, own, far, sent_across, across, partial, product)
+    return exchange(product).reshape(upper_tiles.shape)
 
 
 def solution(mesh):

time: 165 us -> 172 us (1.042)
  blocking collectives: 137 us -> 146 us
  waiting for transfers between devices: 8.47 us -> 0.01 us
  starting transfers between devices: 2.01 us -> 9.08 us
    ppermute x2 -> x5, waiting for transfers between devices: 8.47 us -> 0.01 us  [the longest x2 0.01 us: swap(): lax.ppermute(array, AXES, [(device[p], device[q]) for p, q in places])]
    all_to_all x2, blocking collectives: 137 us -> 146 us  [exchange(): lax.all_to_all(array, 'col', 0, 0, axis_index_groups=[chain(parts)], tile...]
    ppermute x2 -> x5, starting transfers between devices: 2.01 us -> 9.08 us  [the longest x1 5.85 us: shards(): far = lax.ppermute(occupied, AXES, [(p, device[q]) for p, q in facing])]
  transfers between devices with their start and end apart: 2 -> 5, of which waited for: 1 -> 0; matrix products, arithmetic and copies ran while one was open for 0% -> 0% of each run, Pallas kernels for 6% -> 6%
where the time goes in v7:
time: 172 us; the launch traced here: 170 us
  blocking collectives  146 us (85%)
  Pallas kernels  12.7 us (7%)
  starting transfers between devices  9.08 us (5%)
  local copies, waits for them, and re-layouts  2.36 us (1%)
    all_to_all x2, blocking collectives, exchange(): lax.all_to_all(array, 'col', 0, 0, axis_index_groups=[chain(parts)], tile...  146 us
    pallas_call x1, Pallas kernels, square_local(): pl.pallas_call(local_kernel, out_shape=(pltpu.VMEM(tiles.shape, jnp.bfloa...  8.75 us
    ppermute x1, starting transfers between devices, shards(): far = lax.ppermute(occupied, AXES, [(p, device[q]) for p, q in facing])  5.85 us
    pallas_call x2, Pallas kernels, square_border(): pl.pallas_call(functools.partial(border_kernel, across), out_shape=pltpu....  3.71 us
  transfers between devices with their start and end apart: 5, of which 0 were waited for; matrix products, arithmetic and copies ran while one was open for 0% of the time, Pallas kernels for 6%

profile of v7, /device:TPU:34, one launch (start us, length us, event | category | flops | bytes accessed | tf_op | source)
XLA Modules:
  0.0 169.9 jit_solution(3136600631809684837)
XLA Ops:
  0.0 69.5 %all_to_all.10.tiles = bf16[16,8,5,16,256]{4,3,2,1,0:T(8,128)(2,1)S(1)} all-to-all(bf16[16,8,5,16,256]{4,3,2,1,0:T(8,128)(2,1)} %bitcast.4), channel_id=1, replica_groups={{0,1,2,3,4,5,6,7,14,15,12,13,10,11,8,9},{16,17,18,19,20,21,22,23,30,31,..., dimensions={0} | all-to-all | bytes 10485760 | tf_op jit(solution)/shard_map/all_to_all | solution.py:249
  69.5 0.0 copy-start
  69.5 0.2 shard_map.28
  69.7 0.3 collective-permute-start.4
  70.0 1.9 %collective-permute-start.2 = (bf16[16,10,16,256]{3,2,1,0:T(8,128)(2,1)S(1)}, bf16[16,10,16,256]{3,2,1,0:T(8,128)(2,1)S(1)}, u32[]{:S(2)}, u32[]{:S(2)}) collective-permute-start(bf16[16,10,16,256]{3,2,1,0:T(8,128)(2,1)S(1)} %get-tuple-element.10.sent), channel_id=1, source_target_pairs={{1,2},{2,1},{3,4},{4,3},{5,6},{6,5},{7,14},{14,7},{15,12},{12,15},... | collective-permute-start | bytes 3932168 | tf_op jit(solution)/shard_map/ppermute | solution.py:261
  71.9 0.0 copy-done
  71.9 0.7 collective-permute-start
  72.6 0.4 collective-permute-start.3
  73.0 5.8 %collective-permute-start.1 = (s32[4,8]{1,0:T(4,128)S(1)}, s32[4,8]{1,0:T(4,128)S(1)}, u32[]{:S(2)}, u32[]{:S(2)}) collective-permute-start(s32[4,8]{1,0:T(4,128)S(1)} %bitcast.7), channel_id=1, source_target_pairs={{1,2},{2,1},{3,4},{4,3},{5,6},{6,5},{7,14},{8,7},{9,12},{10,15},{1... | collective-permute-start | bytes 392 | tf_op jit(solution)/shard_map/ppermute | solution.py:270
  78.8 0.0 collective-permute-done.occupied
  78.8 8.7 %shard_map.29 = (bf16[16,8,5,16,256]{4,3,2,1,0:T(8,128)(2,1)S(1)}, f32[20,256,256]{2,1,0:T(8,128)S(1)}) custom-call(s32[4,8]{1,0:T(4,128)S(1)} %collective-permute-done.occupied, bf16[16,8,5,16,256]{4,3,2,1,0:T(8,128)(2,1)S(1)} %get-tuple-element.11.tiles), custom_call_target="tpu_custom_call" | custom-call | tf_op jit(solution)/shard_map/pallas_call | solution.py:160
  87.6 0.0 collective-permute-done.3.theirs
  87.6 0.0 collective-permute-done.4.received
  87.6 2.0 %shard_map.30._ = bf16[16,8,5,16,256]{4,3,2,1,0:T(8,128)(2,1)S(1)} custom-call(s32[4,8]{1,0:T(4,128)S(1)} %collective-permute-done.occupied, s32[4,8]{1,0:T(4,128)S(1)} %collective-permute-done.3.theirs, bf16[16,10,16,256]{3,2,1,0:T(8,128)(2,1)S(1)} %get-tuple-element.13.sent, ...), custom_call_target="tpu_custom_call", output_to_operand_aliasing={{}: (5, {})} | custom-call | tf_op jit(solution)/shard_map/pallas_call | solution.py:237
  89.6 0.0 collective-permute-done.1.theirs
  89.6 0.0 collective-permute-done.2.received
  89.6 1.7 shard_map.31
  91.3 76.2 %all_to_all.11 = bf16[16,8,5,16,256]{4,3,2,1,0:T(8,128)(2,1)S(1)} all-to-all(bf16[16,8,5,16,256]{4,3,2,1,0:T(8,128)(2,1)S(1)} %shard_map.31), channel_id=1, replica_groups={{0,1,2,3,4,5,6,7,14,15,12,13,10,11,8,9},{16,17,18,19,20,21,22,23,30,31,..., dimensions={0} | all-to-all | bytes 10485760 | tf_op jit(solution)/shard_map/all_to_all | solution.py:249
  167.5 2.4 %copy.10 = bf16[128,5,16,256]{3,2,1,0:T(8,128)(2,1)} copy(bf16[128,5,16,256]{3,2,1,0:T(8,128)(2,1)S(1)} %bitcast.3) | data formatting | bytes 10485760
Async XLA Ops:
  69.5 2.4 %copy-start = (s32[8,4]{0,1:T(4,128)S(1)}, s32[8,4]{0,1:T(4,128)}, u32[]{:S(2)}) copy-start(s32[8,4]{0,1:T(4,128)} %param.3) | copy-start | bytes 388
  69.7 17.9 %collective-permute-start.4 = (bf16[16,10,16,256]{3,2,1,0:T(8,128)(2,1)S(1)}, bf16[16,10,16,256]{3,2,1,0:T(8,128)(2,1)S(1)}, u32[]{:S(2)}, u32[]{:S(2)}) collective-permute-start(bf16[16,10,16,256]{3,2,1,0:T(8,128)(2,1)S(1)} %get-tuple-element.13.sent), channel_id=1, source_target_pairs={{0,1},{1,0},{2,3},{3,2},{4,5},{5,4},{6,7},{7,6},{14,15},{15,14},{1... | collective-permute-start | bytes 3932168 | tf_op jit(solution)/shard_map/ppermute | solution.py:261
  70.0 19.6 %collective-permute-start.2 = (bf16[16,10,16,256]{3,2,1,0:T(8,128)(2,1)S(1)}, bf16[16,10,16,256]{3,2,1,0:T(8,128)(2,1)S(1)}, u32[]{:S(2)}, u32[]{:S(2)}) collective-permute-start(bf16[16,10,16,256]{3,2,1,0:T(8,128)(2,1)S(1)} %get-tuple-element.10.sent), channel_id=1, source_target_pairs={{1,2},{2,1},{3,4},{4,3},{5,6},{6,5},{7,14},{14,7},{15,12},{12,15},... | collective-permute-start | bytes 3932168 | tf_op jit(solution)/shard_map/ppermute | solution.py:261
  71.9 6.9 %collective-permute-start = (s32[4,8]{1,0:T(4,128)S(1)}, s32[4,8]{1,0:T(4,128)S(1)}, u32[]{:S(2)}, u32[]{:S(2)}) collective-permute-start(s32[4,8]{1,0:T(4,128)S(1)} %bitcast.5), channel_id=1, source_target_pairs={{0,0},{1,1},{2,2},{3,3},{4,4},{5,5},{6,6},{7,7},{8,14},{9,15},{10,... | collective-permute-start | bytes 392 | tf_op jit(solution)/shard_map/ppermute | solution.py:268
  72.6 15.0 %collective-permute-start.3 = (s32[4,8]{1,0:T(4,128)S(1)}, s32[4,8]{1,0:T(4,128)S(1)}, u32[]{:S(2)}, u32[]{:S(2)}) collective-permute-start(s32[4,8]{1,0:T(4,128)S(1)} %bitcast.6), channel_id=1, source_target_pairs={{0,1},{1,0},{2,3},{3,2},{4,5},{5,4},{6,7},{7,6},{8,15},{9,14},{10,... | collective-permute-start | bytes 392 | tf_op jit(solution)/shard_map/ppermute | solution.py:269
  73.0 16.7 %collective-permute-start.1 = (s32[4,8]{1,0:T(4,128)S(1)}, s32[4,8]{1,0:T(4,128)S(1)}, u32[]{:S(2)}, u32[]{:S(2)}) collective-permute-start(s32[4,8]{1,0:T(4,128)S(1)} %bitcast.7), channel_id=1, source_target_pairs={{1,2},{2,1},{3,4},{4,3},{5,6},{6,5},{7,14},{8,7},{9,12},{10,15},{1... | collective-permute-start | bytes 392 | tf_op jit(solution)/shard_map/ppermute | solution.py:270

commit v8 on v6

--- a/solution.py
+++ b/solution.py
@@ -56,6 +56,20 @@
     return odd if across else 1 - odd
 
 
+def pattern(occupied):
+    rows = occupied.shape[1]
+    here = lax.axis_index("row") * lax.axis_size("col") + lax.axis_index("col")
+    there = lax.axis_size("row") * lax.axis_size("col")
+    row = lax.broadcasted_iota(jnp.int32, occupied.shape, 1)
+    d = lax.broadcasted_iota(jnp.int32, occupied.shape, 0) + 1
+    inside = row + d < (there - here) * rows
+    return jnp.where((occupied[...] == 1) & inside, 1.0, 0.0)
+
+
+def spread(mask, row, d, height):
+    return jnp.broadcast_to(mask[d - 1 : d, row : row + 1], (height, BLOCK))
+
+
 def kept_tile(occupied, tiles, row, d):
     tile = tiles[:, row, d]
     return jnp.where(keep(occupied, row, d), tile, jnp.zeros_like(tile))
@@ -65,11 +79,17 @@
     rows = tiles.shape[1]
     odd = next_side(True)
 
+    mask = pattern(occupied)
+
+    def masked(row, d):
+        scale = spread(mask, row, d, tiles.shape[3]).astype(tiles.dtype)
+        return tiles[:, row, d] * scale[None]
+
     def gather(to_next, to_last):
         for slot, (m, d) in enumerate(BELOW):
-            to_next[:, slot] = kept_tile(occupied, tiles, rows - m, d)
+            to_next[:, slot] = masked(rows - m, d)
         for slot, (m, d) in enumerate(ABOVE):
-            to_last[:, slot] = kept_tile(occupied, tiles, m, d) if d else tiles[:, m, d]
+            to_last[:, slot] = masked(m, d) if d else tiles[:, m, d]
 
     @pl.when(odd == 1)
     def _():
@@ -86,7 +106,7 @@
     return pl.pallas_call(
         halo_kernel,
         out_shape=(halo, halo, pltpu.VMEM(tiles.shape, tiles.dtype)),
-        in_specs=[SCALARS, ONCHIP],
+        in_specs=[ONCHIP, ONCHIP],
         out_specs=(ONCHIP,) * 3,
         input_output_aliases={1: 2},
         compiler_params=limit(2),
@@ -154,6 +174,7 @@
     parts, rows, _, height, _ = out.shape
     waiting = partial_tiles(rows)
     upward = next_side(across)
+    mask = pattern(occupied)
 
     def get(ref, slot):
         return ref[:, slot].reshape(BLOCK, BLOCK)
@@ -161,7 +182,7 @@
     def finish(i, e, summed):
         summed = partial[waiting.index((i, e))] + summed
         if e > 0:
-            summed = jnp.where(keep(occupied, i, e), summed, 0.0)
+            summed = jnp.where(spread(mask, i, e, BLOCK) > 0.5, summed, 0.0)
         out[:, i, e] = summed.astype(jnp.bfloat16).reshape(parts, height, BLOCK)
 
     @pl.when(upward == 0)
@@ -204,7 +225,7 @@
     return pl.pallas_call(
         functools.partial(border_kernel, across),
         out_shape=pltpu.VMEM(product.shape, product.dtype),
-        in_specs=[SCALARS] + [ONCHIP] * 4,
+        in_specs=[ONCHIP] * 5,
         out_specs=ONCHIP,
         input_output_aliases={4: 0},
         compiler_params=limit(8),

time: 165 us -> 164 us (level)
  no operation moved by 1% of the time
where the time goes in v8:
time: 164 us; the launch traced here: 162 us
  blocking collectives  138 us (84%)
  Pallas kernels  11.5 us (7%)
  waiting for transfers between devices  8.87 us (5%)
  local copies, waits for them, and re-layouts  2.36 us (1%)
  starting transfers between devices  2.01 us (1%)
    all_to_all x1, blocking collectives, shards(): tiles = lax.all_to_all(tiles, 'col', 0, 0, tiled=True)  70 us
    all_to_all x1, blocking collectives, shards(): product = lax.all_to_all(product, 'col', 0, 0, tiled=True)  67.6 us
    ppermute x1, waiting for transfers between devices, shards(): across = lax.ppermute(sent_across, AXES, swaps(range(1, count - 1, 2)))  8.87 us
    pallas_call x1, Pallas kernels, square_local(): pl.pallas_call(local_kernel, out_shape=(pltpu.VMEM(tiles.shape, jnp.bfloa...  8.74 us
  transfers between devices with their start and end apart: 2, of which 1 were waited for; matrix products, arithmetic and copies ran while one was open for 0% of the time, Pallas kernels for 6%

profile of v8, /device:TPU:34, one launch (start us, length us, event | category | flops | bytes accessed | tf_op | source)
XLA Modules:
  0.0 162.4 jit_solution(13504332993330853001)
XLA Ops:
  0.0 0.0 copy-start
  0.0 70.0 %all_to_all.10.tiles = bf16[16,8,5,16,256]{4,3,2,1,0:T(8,128)(2,1)S(1)} all-to-all(bf16[16,8,5,16,256]{4,3,2,1,0:T(8,128)(2,1)} %bitcast.8), channel_id=1, replica_groups=mesh['row'=8,'col'=16] {'col'}, dimensions={0} | all-to-all | bytes 10485760 | tf_op jit(solution)/shard_map/all_to_all | solution.py:244
  70.0 0.0 copy-done
  70.0 0.3 shard_map.28
  70.3 0.1 collective-permute-start.1
  70.4 1.9 %collective-permute-start = (bf16[16,10,16,256]{3,2,1,0:T(8,128)(2,1)S(1)}, bf16[16,10,16,256]{3,2,1,0:T(8,128)(2,1)S(1)}, u32[]{:S(2)}, u32[]{:S(2)}) collective-permute-start(bf16[16,10,16,256]{3,2,1,0:T(8,128)(2,1)S(1)} %get-tuple-element.10.sent), channel_id=1, source_target_pairs={{1,2},{2,1},{3,4},{4,3},{5,6},{6,5},{7,8},{8,7},{9,10},{10,9},{11,... | collective-permute-start | bytes 3932168 | tf_op jit(solution)/shard_map/ppermute | solution.py:247
  72.3 8.7 %shard_map.29 = (bf16[16,8,5,16,256]{4,3,2,1,0:T(8,128)(2,1)S(1)}, f32[20,256,256]{2,1,0:T(8,128)S(1)}) custom-call(s32[4,8]{1,0:T(4,128)S(1)} %bitcast.4, bf16[16,8,5,16,256]{4,3,2,1,0:T(8,128)(2,1)S(1)} %get-tuple-element.11.tiles), custom_call_target="tpu_custom_call" | custom-call | tf_op jit(solution)/shard_map/pallas_call | solution.py:158
  81.1 0.0 collective-permute-done.1.received
  81.1 1.5 shard_map.30._
  82.6 8.9 %collective-permute-done.received = bf16[16,10,16,256]{3,2,1,0:T(8,128)(2,1)S(1)} collective-permute-done((bf16[16,10,16,256]{3,2,1,0:T(8,128)(2,1)S(1)}, bf16[16,10,16,256]{3,2,1,0:T(8,128)(2,1)S(1)}, u32[]{:S(2)}, u32[]{:S(2)}) %collective-permute-start) | collective-permute-done | bytes 1310752 | tf_op jit(solution)/shard_map/ppermute | solution.py:247
  91.4 1.0 shard_map.31
  92.4 67.6 %all_to_all.11 = bf16[16,8,5,16,256]{4,3,2,1,0:T(8,128)(2,1)S(1)} all-to-all(bf16[16,8,5,16,256]{4,3,2,1,0:T(8,128)(2,1)S(1)} %shard_map.31), channel_id=1, replica_groups=mesh['row'=8,'col'=16] {'col'}, dimensions={0} | all-to-all | bytes 10485760 | tf_op jit(solution)/shard_map/all_to_all | solution.py:252
  160.0 2.4 %copy.10 = bf16[128,5,16,256]{3,2,1,0:T(8,128)(2,1)} copy(bf16[128,5,16,256]{3,2,1,0:T(8,128)(2,1)S(1)} %bitcast.7) | data formatting | bytes 10485760
Async XLA Ops:
  0.0 70.0 %copy-start = (s32[8,4]{0,1:T(4,128)S(1)}, s32[8,4]{0,1:T(4,128)}, u32[]{:S(2)}) copy-start(s32[8,4]{0,1:T(4,128)} %param.3) | copy-start | bytes 388
  70.3 10.8 %collective-permute-start.1 = (bf16[16,10,16,256]{3,2,1,0:T(8,128)(2,1)S(1)}, bf16[16,10,16,256]{3,2,1,0:T(8,128)(2,1)S(1)}, u32[]{:S(2)}, u32[]{:S(2)}) collective-permute-start(bf16[16,10,16,256]{3,2,1,0:T(8,128)(2,1)S(1)} %get-tuple-element.13.sent), channel_id=1, source_target_pairs={{0,1},{1,0},{2,3},{3,2},{4,5},{5,4},{6,7},{7,6},{8,9},{9,8},{10,11... | collective-permute-start | bytes 3932168 | tf_op jit(solution)/shard_map/ppermute | solution.py:248
  70.4 21.0 %collective-permute-start = (bf16[16,10,16,256]{3,2,1,0:T(8,128)(2,1)S(1)}, bf16[16,10,16,256]{3,2,1,0:T(8,128)(2,1)S(1)}, u32[]{:S(2)}, u32[]{:S(2)}) collective-permute-start(bf16[16,10,16,256]{3,2,1,0:T(8,128)(2,1)S(1)} %get-tuple-element.10.sent), channel_id=1, source_target_pairs={{1,2},{2,1},{3,4},{4,3},{5,6},{6,5},{7,8},{8,7},{9,10},{10,9},{11,... | collective-permute-start | bytes 3932168 | tf_op jit(solution)/shard_map/ppermute | solution.py:247

commit v9 on v8

--- a/solution.py
+++ b/solution.py
@@ -12,8 +12,11 @@
 BLOCK = 256
 BAND = 4
 LANES = (2 * BAND + 1) * BLOCK
-BELOW = [(m, d) for m in range(1, BAND + 1) for d in range(m, BAND + 1)]
-ABOVE = [(m, d) for m in range(BAND) for d in range(BAND - m)]
+BELOW = [(m, d) for m in range(1, BAND + 1) for d in range(m + 1, BAND + 1)]
+SPLIT = len(BELOW)
+BELOW += [(m, m) for m in range(1, BAND + 1)]
+ABOVE = [(m, d) for m in range(BAND) for d in range(BAND - 1 - m)]
+ABOVE += [(m, BAND - 1 - m) for m in range(BAND)]
 
 SCALARS = pl.BlockSpec(memory_space=pltpu.SMEM)
 ONCHIP = pl.BlockSpec(memory_space=pltpu.VMEM)
@@ -75,7 +78,13 @@
     return jnp.where(keep(occupied, row, d), tile, jnp.zeros_like(tile))
 
 
-def halo_kernel(occupied, tiles, across, beside, _):
+def pick(refs, slot):
+    if len(refs) == 1 or slot < SPLIT:
+        return refs[0], slot
+    return refs[1], slot - SPLIT
+
+
+def halo_kernel(occupied, tiles, early, late, beside, _):
     rows = tiles.shape[1]
     odd = next_side(True)
 
@@ -87,28 +96,35 @@
 
     def gather(to_next, to_last):
         for slot, (m, d) in enumerate(BELOW):
-            to_next[:, slot] = masked(rows - m, d)
+            put(to_next, slot, masked(rows - m, d))
         for slot, (m, d) in enumerate(ABOVE):
-            to_last[:, slot] = masked(m, d) if d else tiles[:, m, d]
+            put(to_last, slot, masked(m, d) if d else tiles[:, m, d])
+
+    def put(refs, slot, value):
+        ref, at = pick(refs, slot)
+        ref[:, at] = value
 
     @pl.when(odd == 1)
     def _():
-        gather(across, beside)
+        gather((early, late), (beside,))
 
     @pl.when(odd == 0)
     def _():
-        gather(beside, across)
+        gather((beside,), (early, late))
 
 
 def halo_tiles(occupied, tiles):
     parts, _, _, height, width = tiles.shape
-    halo = pltpu.VMEM((parts, len(BELOW), height, width), tiles.dtype)
+    early, late, whole = (
+        pltpu.VMEM((parts, count, height, width), tiles.dtype)
+        for count in (SPLIT, len(BELOW) - SPLIT, len(BELOW))
+    )
     return pl.pallas_call(
         halo_kernel,
-        out_shape=(halo, halo, pltpu.VMEM(tiles.shape, tiles.dtype)),
+        out_shape=(early, late, whole, pltpu.VMEM(tiles.shape, tiles.dtype)),
         in_specs=[ONCHIP, ONCHIP],
-        out_specs=(ONCHIP,) * 3,
-        input_output_aliases={1: 2},
+        out_specs=(ONCHIP,) * 4,
+        input_output_aliases={1: 3},
         compiler_params=limit(2),
     )(occupied, onchip(tiles))
 
@@ -170,14 +186,17 @@
     )(occupied, onchip(tiles))
 
 
-def border_kernel(across, occupied, sent, received, partial, _, out):
+def border_kernel(across, stages, pieces, occupied, *refs):
+    sent, received = refs[: pieces[0]], refs[pieces[0] : sum(pieces)]
+    partial, _, out = refs[sum(pieces) :]
     parts, rows, _, height, _ = out.shape
     waiting = partial_tiles(rows)
     upward = next_side(across)
     mask = pattern(occupied)
 
-    def get(ref, slot):
-        return ref[:, slot].reshape(BLOCK, BLOCK)
+    def get(arrays, slot):
+        ref, at = pick(arrays, slot)
+        return ref[:, at].reshape(BLOCK, BLOCK)
 
     def finish(i, e, summed):
         summed = partial[waiting.index((i, e))] + summed
@@ -192,11 +211,13 @@
                 [get(received, BELOW.index((m, j + m))).T for m in range(BAND - j, 0, -1)],
                 axis=1,
             )
-            for j in range(BAND)
+            for j in range(0 if 1 in stages else 1, BAND)
         }
-        for j in range(BAND):
+        for j in lower:
             depth = (BAND - j) * BLOCK
             for i in range(j + 1):
+                if (0 if i else 1) not in stages:
+                    continue
                 rows_i = lower[i][:, lower[i].shape[1] - depth :]
                 finish(i, j - i, times_transposed(rows_i, lower[j]))
 
@@ -209,10 +230,13 @@
                 return get(received, ABOVE.index((a, b - a)))
             return get(received, ABOVE.index((b, a - b))).T
 
+        size = BAND if 1 in stages else BAND - 1
         square = [
-            jnp.concatenate([corner(a, b) for b in range(BAND)], axis=1) for a in range(BAND)
+            jnp.concatenate([corner(a, b) for b in range(size)], axis=1) for a in range(size)
         ]
         for i in range(rows - BAND, rows):
+            if (1 if i == rows - 1 else 0) not in stages:
+                continue
             reach = i + BAND + 1 - rows
             rows_i = jnp.concatenate(
                 [get(sent, BELOW.index((rows - i, rows + b - i))) for b in range(reach)], axis=1
@@ -221,15 +245,15 @@
                 finish(i, rows + a - i, times_transposed(rows_i, square[a][:, : reach * BLOCK]))
 
 
-def square_border(across, occupied, sent, received, partial, product):
+def square_border(across, stages, occupied, sent, received, partial, product):
     return pl.pallas_call(
-        functools.partial(border_kernel, across),
+        functools.partial(border_kernel, across, stages, (len(sent), len(received))),
         out_shape=pltpu.VMEM(product.shape, product.dtype),
-        in_specs=[ONCHIP] * 5,
+        in_specs=[ONCHIP] * (3 + len(sent) + len(received)),
         out_specs=ONCHIP,
-        input_output_aliases={4: 0},
+        input_output_aliases={2 + len(sent) + len(received): 0},
         compiler_params=limit(8),
-    )(occupied, *(onchip(a) for a in (sent, received, partial, product)))
+    )(occupied, *(onchip(a) for a in (*sent, *received, partial, product)))
 
 
 def swaps(firsts):
@@ -243,12 +267,16 @@
     tiles = upper_tiles.reshape((parts, rows) + upper_tiles.shape[1:])
     tiles = lax.all_to_all(tiles, "col", 0, 0, tiled=True)
     occupied = occupied.T
-    sent_across, sent_beside, tiles = halo_tiles(occupied, tiles)
-    across = lax.ppermute(sent_across, AXES, swaps(range(1, count - 1, 2)))
+    early, late, sent_beside, tiles = halo_tiles(occupied, tiles)
+    facing = swaps(range(1, count - 1, 2))
+    first = lax.ppermute(early, AXES, facing)
+    second = lax.ppermute(late, AXES, facing)
     beside = lax.ppermute(sent_beside, AXES, swaps(range(0, count, 2)))
+    sent = (early, late)
     product, partial = square_local(occupied, tiles)
-    product = square_border(False, occupied, sent_beside, beside, partial, product)
-    product = square_border(True, occupied, sent_across, across, partial, product)
+    product = square_border(False, (0, 1), occupied, (sent_beside,), (beside,), partial, product)
+    product = square_border(True, (0,), occupied, sent, (first,), partial, product)
+    product = square_border(True, (1,), occupied, sent, (first, second), partial, product)
     product = lax.all_to_all(product, "col", 0, 0, tiled=True)
     return product.reshape(upper_tiles.shape)
 

time: 164 us -> 163 us (level)
  waiting for transfers between devices: 8.87 us -> 2.45 us
  starting transfers between devices: 2.01 us -> 7.76 us
    ppermute x1 -> x2, waiting for transfers between devices: 8.87 us -> 2.45 us  [the longest x1 2.45 us: shards(): second = lax.ppermute(late, AXES, facing)]
    ppermute x1 -> x2, starting transfers between devices: 1.92 us -> 7.67 us  [the longest x1 5.75 us: shards(): second = lax.ppermute(late, AXES, facing)]
  transfers between devices with their start and end apart: 2 -> 3, of which waited for: 1 -> 1; matrix products, arithmetic and copies ran while one was open for 0% -> 0% of each run, Pallas kernels for 6% -> 7%
where the time goes in v9:
time: 163 us; the launch traced here: 162 us
  blocking collectives  137 us (84%)
  Pallas kernels  11.8 us (7%)
  starting transfers between devices  7.76 us (5%)
  waiting for transfers between devices  2.45 us (2%)
  local copies, waits for them, and re-layouts  2.36 us (1%)
    all_to_all x1, blocking collectives, shards(): tiles = lax.all_to_all(tiles, 'col', 0, 0, tiled=True)  70 us
    all_to_all x1, blocking collectives, shards(): product = lax.all_to_all(product, 'col', 0, 0, tiled=True)  67.3 us
    pallas_call x1, Pallas kernels, square_local(): pl.pallas_call(local_kernel, out_shape=(pltpu.VMEM(tiles.shape, jnp.bfloa...  8.74 us
    ppermute x1, starting transfers between devices, shards(): second = lax.ppermute(late, AXES, facing)  5.75 us
  transfers between devices with their start and end apart: 3, of which 1 were waited for; matrix products, arithmetic and copies ran while one was open for 0% of the time, Pallas kernels for 7%

profile of v9, /device:TPU:34, one launch (start us, length us, event | category | flops | bytes accessed | tf_op | source)
XLA Modules:
  0.0 161.8 jit_solution(16963714272276736454)
XLA Ops:
  0.0 0.0 copy-start
  0.0 70.0 %all_to_all.10.tiles = bf16[16,8,5,16,256]{4,3,2,1,0:T(8,128)(2,1)S(1)} all-to-all(bf16[16,8,5,16,256]{4,3,2,1,0:T(8,128)(2,1)} %bitcast.9), channel_id=1, replica_groups=mesh['row'=8,'col'=16] {'col'}, dimensions={0} | all-to-all | bytes 10485760 | tf_op jit(solution)/shard_map/all_to_all | solution.py:268
  70.0 0.0 copy-done
  70.0 0.3 shard_map.28
  70.3 0.1 collective-permute-start.2
  70.4 1.9 %collective-permute-start = (bf16[16,6,16,256]{3,2,1,0:T(8,128)(2,1)S(1)}, bf16[16,6,16,256]{3,2,1,0:T(8,128)(2,1)S(1)}, u32[]{:S(2)}, u32[]{:S(2)}) collective-permute-start(bf16[16,6,16,256]{3,2,1,0:T(8,128)(2,1)S(1)} %get-tuple-element.11.refs_0_), channel_id=1, source_target_pairs={{1,2},{2,1},{3,4},{4,3},{5,6},{6,5},{7,8},{8,7},{9,10},{10,9},{11,... | collective-permute-start | bytes 2359304 | tf_op jit(solution)/shard_map/ppermute | solution.py:272
  72.3 5.8 %collective-permute-start.1 = (bf16[16,4,16,256]{3,2,1,0:T(8,128)(2,1)S(1)}, bf16[16,4,16,256]{3,2,1,0:T(8,128)(2,1)S(1)}, u32[]{:S(2)}, u32[]{:S(2)}) collective-permute-start(bf16[16,4,16,256]{3,2,1,0:T(8,128)(2,1)S(1)} %get-tuple-element.12.refs_1_), channel_id=1, source_target_pairs={{1,2},{2,1},{3,4},{4,3},{5,6},{6,5},{7,8},{8,7},{9,10},{10,9},{11,... | collective-permute-start | bytes 1572872 | tf_op jit(solution)/shard_map/ppermute | solution.py:273
  78.1 8.7 %shard_map.29 = (bf16[16,8,5,16,256]{4,3,2,1,0:T(8,128)(2,1)S(1)}, f32[20,256,256]{2,1,0:T(8,128)S(1)}) custom-call(s32[4,8]{1,0:T(4,128)S(1)} %bitcast.4, bf16[16,8,5,16,256]{4,3,2,1,0:T(8,128)(2,1)S(1)} %get-tuple-element.13.tiles), custom_call_target="tpu_custom_call" | custom-call | tf_op jit(solution)/shard_map/pallas_call | solution.py:174
  86.8 0.0 collective-permute-done.2.refs_1_
  86.8 1.5 shard_map.30.refs_4_
  88.3 0.0 collective-permute-done.refs_2_
  88.3 0.6 shard_map.31.refs_5_
  89.0 2.4 %collective-permute-done.1.refs_3_ = bf16[16,4,16,256]{3,2,1,0:T(8,128)(2,1)S(1)} collective-permute-done((bf16[16,4,16,256]{3,2,1,0:T(8,128)(2,1)S(1)}, bf16[16,4,16,256]{3,2,1,0:T(8,128)(2,1)S(1)}, u32[]{:S(2)}, u32[]{:S(2)}) %collective-permute-start.1) | collective-permute-done | bytes 524320 | tf_op jit(solution)/shard_map/ppermute | solution.py:273
  91.4 0.6 shard_map.32
  92.1 67.3 %all_to_all.11 = bf16[16,8,5,16,256]{4,3,2,1,0:T(8,128)(2,1)S(1)} all-to-all(bf16[16,8,5,16,256]{4,3,2,1,0:T(8,128)(2,1)S(1)} %shard_map.32), channel_id=1, replica_groups=mesh['row'=8,'col'=16] {'col'}, dimensions={0} | all-to-all | bytes 10485760 | tf_op jit(solution)/shard_map/all_to_all | solution.py:280
  159.4 2.4 %copy.12 = bf16[128,5,16,256]{3,2,1,0:T(8,128)(2,1)} copy(bf16[128,5,16,256]{3,2,1,0:T(8,128)(2,1)S(1)} %bitcast.8) | data formatting | bytes 10485760
Async XLA Ops:
  0.0 70.0 %copy-start = (s32[8,4]{0,1:T(4,128)S(1)}, s32[8,4]{0,1:T(4,128)}, u32[]{:S(2)}) copy-start(s32[8,4]{0,1:T(4,128)} %param.3) | copy-start | bytes 388
  70.3 16.5 %collective-permute-start.2 = (bf16[16,10,16,256]{3,2,1,0:T(8,128)(2,1)S(1)}, bf16[16,10,16,256]{3,2,1,0:T(8,128)(2,1)S(1)}, u32[]{:S(2)}, u32[]{:S(2)}) collective-permute-start(bf16[16,10,16,256]{3,2,1,0:T(8,128)(2,1)S(1)} %get-tuple-element.15.refs_0_), channel_id=1, source_target_pairs={{0,1},{1,0},{2,3},{3,2},{4,5},{5,4},{6,7},{7,6},{8,9},{9,8},{10,11... | collective-permute-start | bytes 3932168 | tf_op jit(solution)/shard_map/ppermute | solution.py:274
  70.4 17.9 %collective-permute-start = (bf16[16,6,16,256]{3,2,1,0:T(8,128)(2,1)S(1)}, bf16[16,6,16,256]{3,2,1,0:T(8,128)(2,1)S(1)}, u32[]{:S(2)}, u32[]{:S(2)}) collective-permute-start(bf16[16,6,16,256]{3,2,1,0:T(8,128)(2,1)S(1)} %get-tuple-element.11.refs_0_), channel_id=1, source_target_pairs={{1,2},{2,1},{3,4},{4,3},{5,6},{6,5},{7,8},{8,7},{9,10},{10,9},{11,... | collective-permute-start | bytes 2359304 | tf_op jit(solution)/shard_map/ppermute | solution.py:272
  72.3 19.1 %collective-permute-start.1 = (bf16[16,4,16,256]{3,2,1,0:T(8,128)(2,1)S(1)}, bf16[16,4,16,256]{3,2,1,0:T(8,128)(2,1)S(1)}, u32[]{:S(2)}, u32[]{:S(2)}) collective-permute-start(bf16[16,4,16,256]{3,2,1,0:T(8,128)(2,1)S(1)} %get-tuple-element.12.refs_1_), channel_id=1, source_target_pairs={{1,2},{2,1},{3,4},{4,3},{5,6},{6,5},{7,8},{8,7},{9,10},{10,9},{11,... | collective-permute-start | bytes 1572872 | tf_op jit(solution)/shard_map/ppermute | solution.py:273
